TPU v7x, 128 devices: a whole 4x4x4 slice. The times are simulated.
128 devices in a mesh: grp: 8 (over y, core), dev: 16 (over z, x).
Axes of the slice: x: 4, y: 4, z: 4, core: 2. Of those that a mesh axis runs over, the one named last changes fastest.
Arguments:
- basis_old: float32 [128, 2097152], P(None, ('grp', 'dev')), as said below
- values_old: float32 [128], replicated, may hold values from 1 to 4
- snapshots: float32 [2, 64, 2097152], P(None, None, ('grp', 'dev'))
- wet_counts: int32 [128], P(('grp', 'dev')), may hold values from 1 to 128, as said below
Outputs:
- basis_new: float32 [128, 2097152], P(None, ('grp', 'dev'))
- values_new: float32 [128], replicated
Inputs may be any that keep to these rules, and one draw needn't show every extreme that they name: `wet_counts`: every device has at least one wet block, and some device has all 128 blocks wet. basis_old is zero on every cell that wet_mask marks dry.
All inputs are finite; a program needn't handle non-finite values.
Results may differ from a plain program's by a relative error of at most 0.0003.
Values sent between devices are 32-bit elements; how exact they have to be, the bound alone decides.
No kernel may reach another device: no remote copies, remote signals or barrier semaphores. Data moves between devices by JAX's collectives and lax.ppermute only.
A program may use at most 128 MiB of HBM per device.

v0:
```python
import jax
import jax.numpy as jnp
from jax import lax
from jax.sharding import PartitionSpec as P

BLOCK = 128
SWEEPS = 3


def matmul_nn(left_op, right_op):
    return jnp.dot(
        left_op, right_op, precision=lax.Precision.HIGHEST, preferred_element_type=jnp.float32
    )


def matmul_nt(left_op, right_op):
    return lax.dot_general(
        left_op,
        right_op,
        (((1,), (1,)), ((), ())),
        precision=lax.Precision.HIGHEST,
        preferred_element_type=jnp.float32,
    )


def matmul_tn(left_op, right_op):
    return lax.dot_general(
        left_op,
        right_op,
        (((0,), (0,)), ((), ())),
        precision=lax.Precision.HIGHEST,
        preferred_element_type=jnp.float32,
    )


def assemble(values, project, factor):
    upper_block = jnp.concatenate([jnp.diag(values), project], 1)
    bottom = jnp.concatenate(
        [jnp.zeros((factor.shape[0], values.shape[0]), jnp.float32), factor.T], 1
    )
    return jnp.concatenate([upper_block, bottom], 0)


def refine(core_matrix, rank_width):
    frame_now = jnp.eye(core_matrix.shape[0], rank_width, dtype=jnp.float32)
    for repeat in range(SWEEPS):
        grown_cols = matmul_nn(core_matrix, matmul_tn(core_matrix, frame_now))
        lower_part = jnp.linalg.cholesky(matmul_tn(grown_cols, grown_cols))
        frame_now = jax.scipy.linalg.solve_triangular(lower_part, grown_cols.T, lower=True).T
    return frame_now


def per_device(basis_old, values_old, snapshots, wet_counts):
    counts = lax.all_gather(wet_counts, ("grp", "dev"), axis=0, tiled=True)
    wet_total = jnp.sum(counts).astype(jnp.float32) * BLOCK
    rows_here = basis_old.shape[1]
    wet_mask = (lax.iota(jnp.int32, rows_here) // BLOCK < wet_counts[0]).astype(jnp.float32)
    rank_width = basis_old.shape[0]

    def update_one(state_pair, snapshot):
        current, values = state_pair
        columns = snapshot * wet_mask[None, :]
        project = lax.psum(matmul_nt(current, columns), ("grp", "dev")) / wet_total
        remainder = columns - matmul_tn(project, current)
        gram = lax.psum(matmul_nt(remainder, remainder), ("grp", "dev")) / wet_total
        factor = jnp.linalg.cholesky(gram)
        fresh_rows = jax.scipy.linalg.solve_triangular(factor, remainder, lower=True)
        core_matrix = assemble(values, project, factor)
        frame_now = refine(core_matrix, rank_width)
        stacked = jnp.concatenate([current, fresh_rows], 0)
        new_basis = matmul_tn(frame_now, stacked)
        rotated = matmul_tn(frame_now, core_matrix)
        new_values = jnp.sqrt(jnp.sum(rotated * rotated, axis=1))
        return ((new_basis, new_values), None)

    (current, values), _ = lax.scan(update_one, (basis_old, values_old), snapshots)
    return (current, values)


def solution(mesh):
    return jax.shard_map(
        per_device,
        mesh=mesh,
        in_specs=(P(None, ("grp", "dev")), P(), P(None, None, ("grp", "dev")), P(("grp", "dev"))),
        out_specs=(P(None, ("grp", "dev")), P()),
        check_vma=False,
    )
```

profile of v0, /device:TPU:1, one launch (start us, length us, event | category | flops | bytes accessed | tf_op | source)
XLA Modules:
  0.0 607.9 jit_solution(14972124603921048518)
XLA Ops:
  0.6 7.6 %copy.42 = f32[128,16384]{1,0:T(8,128)} copy(f32[128,16384]{1,0:T(8,128)} %param.9) | data formatting | bytes 16777216
  9.0 68.6 %all-reduce.1 = s32[128]{0:T(128)S(1)} all-reduce(s32[128]{0:T(128)S(1)} %dynamic-update-slice.5), channel_id=1, replica_groups=mesh['grp'=8,'dev'=16] {'grp','dev'}, use_global_device_ids=true, to_apply=%add.1 | all-reduce | flops 128 | bytes 1024
  77.6 0.7 reduce_sum.18
  79.0 527.8 %while.13 = (s32[]{:T(128)}, f32[128,16384]{1,0:T(8,128)}, f32[128]{0:T(128)S(1)}, f32[2,64,16384]{2,1,0:T(8,128)}, f32[]{:T(128)}, /*index=5*/s32[]{:T(128)}, s32[]{:T(128)}) while((s32[]{:T(128)}, f32[128,16384]{1,0:T(8,128)}, f32[128]{0:T(128)S(1)}, f32[2,64,16384]{2,1,0:T(8,128)}, f32[]{:T(128)}, /*index=5*/s32[]{:T(128)}, ...), condition=%wide.region_9.12_spmd.clone, body=%wide.region_1.11_spmd.clone.sunk | while | flops 10294632448 | bytes 169318064 | solution.py:76
  79.3 3.5 copy.45
  82.8 1.6 fusion.152
  84.4 2.7 copy-done
  87.1 1.0 copy-done.2
  88.1 8.8 %fusion.153 = f32[128,64]{0,1:T(8,128)S(1)} fusion(f32[128,16384]{1,0:T(8,128)S(1)} %copy.45, f32[2,64,16384]{2,1,0:T(8,128)S(1)} %copy-done.2, s32[]{:T(128)} %get-tuple-element.116, f32[16384]{0:T(1024)S(1)} %fusion.152), kind=kOutput, calls=%fused_computation.11.clone.1 | convolution fusion | flops 1611661312 | bytes 12681220 | tf_op jit(solution)/shard_map/while/body/eval_jaxpr/dot_general | solution.py:17
  96.9 62.9 %psum.18 = f32[128,64]{0,1:T(8,128)S(1)} all-reduce(f32[128,64]{0,1:T(8,128)S(1)} %fusion.153), channel_id=1, replica_groups=mesh['grp'=8,'dev'=16] {'grp','dev'}, use_global_device_ids=true, to_apply=%region_2.2 | all-reduce | flops 8192 | bytes 65536 | tf_op jit(solution)/shard_map/while/body/eval_jaxpr/psum | solution.py:63
  159.8 7.8 %convolution_subtract_fusion.2 = f32[64,16384]{1,0:T(8,128)S(1)} fusion(f32[128,64]{0,1:T(8,128)S(1)} %broadcast_divide_fusion.4, f32[128,16384]{1,0:T(8,128)} %copy-done, f32[2,64,16384]{2,1,0:T(8,128)} %get-tuple-element.126, s32[]{:T(128)} %get-tuple-element.116, f32[16384]{0:T(1024)S(1)} %fusion.152), kind=kOutput, calls=%fused_computation.1.clone.1 | convolution fusion | flops 1612709888 | bytes 16875524 | tf_op jit(solution)/shard_map/while/body/eval_jaxpr/dot_general | solution.py:27
  167.6 2.0 copy-done.1
  169.6 3.4 fusion.154
  173.0 64.8 %psum.19 = f32[64,64]{0,1:T(8,128)S(1)} all-reduce(f32[64,64]{0,1:T(8,128)S(1)} %fusion.154), channel_id=1, replica_groups=mesh['grp'=8,'dev'=16] {'grp','dev'}, use_global_device_ids=true, to_apply=%region_3.3 | all-reduce | flops 4096 | bytes 32768 | tf_op jit(solution)/shard_map/while/body/eval_jaxpr/psum | solution.py:65
  238.0 5.8 cholesky.285
  243.9 0.7 compare_reduce_fusion.8
  246.7 11.7 %cholesky.286 = f32[128,128]{1,0:T(8,128)S(1)} custom-call(f32[128,128]{1,0:T(8,128)S(1)} %fusion.160), custom_call_target="Cholesky" | custom-call | tf_op jit(solution)/shard_map/while/body/eval_jaxpr/jit(cholesky)/cholesky | solution.py:48
  258.4 0.7 compare_reduce_fusion.9
  259.7 9.8 %custom-call.22 = f32[1,128,128]{1,2,0:T(8,128)S(1)} custom-call(f32[1,128,128]{2,1,0:T(8,128)S(1)} %fusion.162), custom_call_target="InvertDiagBlocksLowerTriangular" | custom-call | tf_op jit(solution)/shard_map/while/body/eval_jaxpr/jit(_solve_triangular)/triangular_solve | solution.py:49
  271.3 11.9 %cholesky.287 = f32[128,128]{1,0:T(8,128)S(1)} custom-call(f32[128,128]{1,0:T(8,128)S(1)} %fusion.167), custom_call_target="Cholesky" | custom-call | tf_op jit(solution)/shard_map/while/body/eval_jaxpr/jit(cholesky)/cholesky | solution.py:48
  283.2 0.7 compare_reduce_fusion.10
  284.5 9.8 %custom-call.23 = f32[1,128,128]{1,2,0:T(8,128)S(1)} custom-call(f32[1,128,128]{2,1,0:T(8,128)S(1)} %fusion.169), custom_call_target="InvertDiagBlocksLowerTriangular" | custom-call | tf_op jit(solution)/shard_map/while/body/eval_jaxpr/jit(_solve_triangular)/triangular_solve | solution.py:49
  296.0 11.7 %cholesky.288 = f32[128,128]{1,0:T(8,128)S(1)} custom-call(f32[128,128]{1,0:T(8,128)S(1)} %fusion.174), custom_call_target="Cholesky" | custom-call | tf_op jit(solution)/shard_map/while/body/eval_jaxpr/jit(cholesky)/cholesky | solution.py:48
  309.1 9.8 %custom-call.24 = f32[1,128,128]{1,2,0:T(8,128)S(1)} custom-call(f32[1,128,128]{2,1,0:T(8,128)S(1)} %fusion.175), custom_call_target="InvertDiagBlocksLowerTriangular" | custom-call | tf_op jit(solution)/shard_map/while/body/eval_jaxpr/jit(_solve_triangular)/triangular_solve | solution.py:49
  319.7 4.9 custom-call.25
  324.6 5.6 fusion.177
  330.2 12.3 %fusion.178 = f32[128,16384]{1,0:T(8,128)} fusion(f32[128,192]{0,1:T(8,128)S(1)} %fusion.176, f32[64,16384]{1,0:T(8,128)S(1)} %fusion.177, f32[128,16384]{1,0:T(8,128)} %copy-done), kind=kOutput, calls=%fused_computation.2.clone.1 | convolution fusion | flops 4834983936 | bytes 21069824 | tf_op jit(solution)/shard_map/while/body/eval_jaxpr/dot_general | solution.py:27
  342.8 3.5 copy.45
  346.3 1.6 fusion.152
  347.9 2.7 copy-done
  350.6 1.0 copy-done.2
  351.6 8.8 %fusion.153 = f32[128,64]{0,1:T(8,128)S(1)} fusion(f32[128,16384]{1,0:T(8,128)S(1)} %copy.45, f32[2,64,16384]{2,1,0:T(8,128)S(1)} %copy-done.2, s32[]{:T(128)} %get-tuple-element.116, f32[16384]{0:T(1024)S(1)} %fusion.152), kind=kOutput, calls=%fused_computation.11.clone.1 | convolution fusion | flops 1611661312 | bytes 12681220 | tf_op jit(solution)/shard_map/while/body/eval_jaxpr/dot_general | solution.py:17
  360.4 63.0 %psum.18 = f32[128,64]{0,1:T(8,128)S(1)} all-reduce(f32[128,64]{0,1:T(8,128)S(1)} %fusion.153), channel_id=1, replica_groups=mesh['grp'=8,'dev'=16] {'grp','dev'}, use_global_device_ids=true, to_apply=%region_2.2 | all-reduce | flops 8192 | bytes 65536 | tf_op jit(solution)/shard_map/while/body/eval_jaxpr/psum | solution.py:63
  423.4 7.8 %convolution_subtract_fusion.2 = f32[64,16384]{1,0:T(8,128)S(1)} fusion(f32[128,64]{0,1:T(8,128)S(1)} %broadcast_divide_fusion.4, f32[128,16384]{1,0:T(8,128)} %copy-done, f32[2,64,16384]{2,1,0:T(8,128)} %get-tuple-element.126, s32[]{:T(128)} %get-tuple-element.116, f32[16384]{0:T(1024)S(1)} %fusion.152), kind=kOutput, calls=%fused_computation.1.clone.1 | convolution fusion | flops 1612709888 | bytes 16875524 | tf_op jit(solution)/shard_map/while/body/eval_jaxpr/dot_general | solution.py:27
  431.2 2.0 copy-done.1
  433.2 3.4 fusion.154
  436.6 64.4 %psum.19 = f32[64,64]{0,1:T(8,128)S(1)} all-reduce(f32[64,64]{0,1:T(8,128)S(1)} %fusion.154), channel_id=1, replica_groups=mesh['grp'=8,'dev'=16] {'grp','dev'}, use_global_device_ids=true, to_apply=%region_3.3 | all-reduce | flops 4096 | bytes 32768 | tf_op jit(solution)/shard_map/while/body/eval_jaxpr/psum | solution.py:65
  501.1 5.8 cholesky.285
  507.0 0.7 compare_reduce_fusion.8
  509.8 11.7 %cholesky.286 = f32[128,128]{1,0:T(8,128)S(1)} custom-call(f32[128,128]{1,0:T(8,128)S(1)} %fusion.160), custom_call_target="Cholesky" | custom-call | tf_op jit(solution)/shard_map/while/body/eval_jaxpr/jit(cholesky)/cholesky | solution.py:48
  522.8 9.8 %custom-call.22 = f32[1,128,128]{1,2,0:T(8,128)S(1)} custom-call(f32[1,128,128]{2,1,0:T(8,128)S(1)} %fusion.162), custom_call_target="InvertDiagBlocksLowerTriangular" | custom-call | tf_op jit(solution)/shard_map/while/body/eval_jaxpr/jit(_solve_triangular)/triangular_solve | solution.py:49
  534.4 11.9 %cholesky.287 = f32[128,128]{1,0:T(8,128)S(1)} custom-call(f32[128,128]{1,0:T(8,128)S(1)} %fusion.167), custom_call_target="Cholesky" | custom-call | tf_op jit(solution)/shard_map/while/body/eval_jaxpr/jit(cholesky)/cholesky | solution.py:48
  547.6 9.8 %custom-call.23 = f32[1,128,128]{1,2,0:T(8,128)S(1)} custom-call(f32[1,128,128]{2,1,0:T(8,128)S(1)} %fusion.169), custom_call_target="InvertDiagBlocksLowerTriangular" | custom-call | tf_op jit(solution)/shard_map/while/body/eval_jaxpr/jit(_solve_triangular)/triangular_solve | solution.py:49
  559.2 11.7 %cholesky.288 = f32[128,128]{1,0:T(8,128)S(1)} custom-call(f32[128,128]{1,0:T(8,128)S(1)} %fusion.174), custom_call_target="Cholesky" | custom-call | tf_op jit(solution)/shard_map/while/body/eval_jaxpr/jit(cholesky)/cholesky | solution.py:48
  572.3 9.8 %custom-call.24 = f32[1,128,128]{1,2,0:T(8,128)S(1)} custom-call(f32[1,128,128]{2,1,0:T(8,128)S(1)} %fusion.175), custom_call_target="InvertDiagBlocksLowerTriangular" | custom-call | tf_op jit(solution)/shard_map/while/body/eval_jaxpr/jit(_solve_triangular)/triangular_solve | solution.py:49
  582.8 4.9 custom-call.25
  587.7 5.8 fusion.177
  593.6 12.3 %fusion.178 = f32[128,16384]{1,0:T(8,128)} fusion(f32[128,192]{0,1:T(8,128)S(1)} %fusion.176, f32[64,16384]{1,0:T(8,128)S(1)} %fusion.177, f32[128,16384]{1,0:T(8,128)} %copy-done), kind=kOutput, calls=%fused_computation.2.clone.1 | convolution fusion | flops 4834983936 | bytes 21069824 | tf_op jit(solution)/shard_map/while/body/eval_jaxpr/dot_general | solution.py:27
  (86 shorter events, 20.0 us)
Async XLA Ops:
  0.6 78.4 %copy-start.4 = (f32[128]{0:T(128)S(1)}, f32[128]{0:T(128)}, u32[]{:S(2)}) copy-start(f32[128]{0:T(128)} %param.10) | copy-start | bytes 1540
  79.3 8.8 %copy-start.2 = (f32[2,64,16384]{2,1,0:T(8,128)S(1)}, f32[2,64,16384]{2,1,0:T(8,128)}, u32[]{:S(2)}) copy-start(f32[2,64,16384]{2,1,0:T(8,128)} %get-tuple-element.126) | copy-start | bytes 25165828 | tf_op jit(solution)/shard_map/while
  82.8 4.3 copy-start
  167.6 2.0 copy-start.1
  342.8 8.8 %copy-start.2 = (f32[2,64,16384]{2,1,0:T(8,128)S(1)}, f32[2,64,16384]{2,1,0:T(8,128)}, u32[]{:S(2)}) copy-start(f32[2,64,16384]{2,1,0:T(8,128)} %get-tuple-element.126) | copy-start | bytes 25165828 | tf_op jit(solution)/shard_map/while
  346.3 4.3 copy-start
  431.2 2.0 copy-start.1
  606.9 0.5 copy-start.3
where the time goes:
time: 611 us; the launch traced here: 608 us
  blocking collectives  324 us (53%)
  other arithmetic  166 us (27%)
  matrix products  86 us (14%)
  local copies, waits for them, and re-layouts  27.7 us (5%)
    psum x2, blocking collectives, update_one(): gram = lax.psum(matmul_nt(remainder, remainder), ('grp', 'dev')) / wet_total  129 us
    psum x2, blocking collectives, update_one(): project = lax.psum(matmul_nt(current, columns), ('grp', 'dev')) / wet_total  126 us
    another operation x18, other arithmetic, refine(): lower_part = jnp.linalg.cholesky(matmul_tn(grown_cols, grown_cols))  74.8 us
    unnamed x1, blocking collectives  68.6 us
    another operation x12, other arithmetic, refine(): jax.scipy.linalg.solve_triangular(lower_part, grown_cols.T, lower=True)  62.7 us
    dot_general x18, matrix products, matmul_tn(): lax.dot_general(left_op, right_op, (((0,), (0,)), ((), ())), precision=la...  46.3 us
    dot_general x4, matrix products, matmul_nt(): lax.dot_general(left_op, right_op, (((1,), (1,)), ((), ())), precision=la...  24.4 us
    while x16, local copies, waits for them, and re-layouts  18.6 us

commit v1 on v0

v1 whole, which is shorter than its diff:
```python
import functools

import jax
import jax.numpy as jnp
from jax import lax
from jax.experimental import pallas as pl
from jax.experimental.pallas import tpu as pltpu
from jax.sharding import PartitionSpec as P

BLOCK = 128
SWEEPS = 3
MODES = 128
CHUNK = 2048
F32 = jnp.float32
BF16 = jnp.bfloat16
HIGHEST = lax.Precision.HIGHEST


def dot_nn(left_op, right_op, precision=None):
    return lax.dot_general(
        left_op, right_op, (((1,), (0,)), ((), ())), precision=precision, preferred_element_type=F32
    )


def dot_nt(left_op, right_op, precision=None):
    return lax.dot_general(
        left_op, right_op, (((1,), (1,)), ((), ())), precision=precision, preferred_element_type=F32
    )


def load_split(step, wet, basis_ref, snap_ref):
    width = basis_ref.shape[1]
    cell = lax.broadcasted_iota(jnp.int32, snap_ref.shape, 1) + step * width
    columns = jnp.where(cell < wet * BLOCK, snap_ref[...], 0.0)
    rows = jnp.concatenate([basis_ref[...], columns], 0)
    lead = rows.astype(BF16)
    rest = (rows - lead.astype(F32)).astype(BF16)
    return lead, rest


def gram_kernel(info_ref, basis_ref, snap_ref, mine_ref, other_ref, even_acc, cross_acc):
    step = pl.program_id(0)

    @pl.when(step == 0)
    def _():
        even_acc[...] = jnp.zeros_like(even_acc)
        cross_acc[...] = jnp.zeros_like(cross_acc)

    lead, rest = load_split(step, info_ref[0], basis_ref, snap_ref)
    even_acc[...] += dot_nt(lead, lead) + dot_nt(rest, rest)
    cross_acc[...] += dot_nt(lead, rest)

    @pl.when(step == pl.num_programs(0) - 1)
    def _():
        cross = cross_acc[...]
        gram = even_acc[...] + (cross + cross.T)
        row = lax.broadcasted_iota(jnp.int32, (MODES, MODES), 0)
        lane = lax.broadcasted_iota(jnp.int32, (MODES, MODES), 1)
        snap_gram = gram[MODES:, MODES:]
        diagonal = jnp.sum(jnp.where(row == lane, snap_gram, 0.0), 0, keepdims=True)
        extra = jnp.where(
            lax.broadcasted_iota(jnp.int32, (8, MODES), 0) == 0,
            jnp.broadcast_to(diagonal, (8, MODES)),
            jnp.full((8, MODES), info_ref[0].astype(F32)),
        )
        symmetric = jnp.concatenate(
            [jnp.where(lane <= row, gram[:MODES, :MODES], snap_gram), extra], 0
        )
        mixed = jnp.concatenate([gram[:MODES, MODES:], jnp.zeros((8, MODES), F32)], 0)
        first = info_ref[1] == 0
        mine_ref[...] = jnp.where(first, symmetric, mixed)
        other_ref[...] = jnp.where(first, mixed, symmetric)


def lane_of(tile, index):
    return jnp.broadcast_to(tile[:, index : index + 1], tile.shape)


def row_of(tile, index):
    return jnp.broadcast_to(tile[index : index + 1, :], tile.shape)


def tree_sum(terms):
    while len(terms) > 1:
        terms = [
            terms[i] + terms[i + 1] if i + 1 < len(terms) else terms[i]
            for i in range(0, len(terms), 2)
        ]
    return terms[0]


def inverse_factor(tiles, base):
    sub = lax.broadcasted_iota(jnp.int32, (8, MODES), 0)
    lane = lax.broadcasted_iota(jnp.int32, (8, MODES), 1)
    tiles = list(tiles)
    finished = []
    for block in range(len(tiles)):
        start = base + 8 * block
        tile = tiles[block]
        cols = [lane_of(tile, start + j) for j in range(8)]
        pivots = None
        for k in range(8):
            pivot = row_of(cols[k], k)
            pivots = pivot if pivots is None else jnp.where(sub >= k, pivot, pivots)
            unit = jnp.where(sub == k, 1.0, 0.0)
            if k < 7:
                scale = jnp.where(sub > k, cols[k], 0.0) * (1.0 / pivot)
                for j in range(8):
                    if j != k:
                        cols[j] = cols[j] - scale * row_of(cols[j], k)
                cols[k] = unit - scale
            else:
                cols[k] = unit
        root = lax.rsqrt(pivots)
        cols = [c * root for c in cols]
        inside = (lane >= start) & (lane < start + 8)
        tile = jnp.where(inside, jnp.where(lane - start == sub, 1.0, 0.0), tile)
        done = tree_sum([cols[c] * row_of(tile, c) for c in range(8)])
        finished.append(jnp.where(lane < start + 8, done, 0.0))
        if block + 1 == len(tiles):
            break
        done_rows = [row_of(done, r) for r in range(8)]
        update = [
            tree_sum([row_of(cols[c], r) * done_rows[r] for r in range(c, 8)]) for c in range(8)
        ]
        for other in range(block + 1, len(tiles)):
            kept = jnp.where(inside, 0.0, tiles[other])
            tiles[other] = kept - tree_sum(
                [lane_of(tiles[other], start + c) * update[c] for c in range(8)]
            )
    return finished


def core_kernel(batches, parity_ref, mine_ref, other_ref, values_ref, coeff_ref, out_ref, frame, gram_buf):
    first = parity_ref[0] == 0
    mine, other = mine_ref[...], other_ref[...]
    symmetric = jnp.where(first, mine, other)
    mixed = jnp.where(first, other, mine)[:MODES]
    row = lax.broadcasted_iota(jnp.int32, (MODES, MODES), 0)
    lane = lax.broadcasted_iota(jnp.int32, (MODES, MODES), 1)
    identity = jnp.where(row == lane, 1.0, 0.0)
    wet_total = symmetric[MODES + 1 : MODES + 2, 0:1] * BLOCK
    weight = 1.0 / wet_total
    diagonal = symmetric[MODES : MODES + 1, :] * weight
    symmetric = symmetric[:MODES] * weight
    flipped = symmetric.T
    basis_gram = jnp.where(lane <= row, symmetric, flipped)
    snap_gram = jnp.where(lane > row, symmetric, jnp.where(lane == row, diagonal, flipped))
    mixed = mixed * weight
    gram_all = jnp.concatenate(
        [
            jnp.concatenate([basis_gram, mixed], 1),
            jnp.concatenate([mixed.T, snap_gram], 1),
        ],
        0,
    )
    coeff = jnp.concatenate([identity, jnp.zeros((MODES, MODES), F32)], 1)
    squares = values_ref[...] * values_ref[...]
    width = MODES // batches
    for batch in range(batches):
        chosen = (lane >= batch * width) & (lane < (batch + 1) * width)
        if batch == 0:
            project = jnp.where(chosen, mixed, 0.0)
        else:
            project = jnp.where(chosen, dot_nn(coeff, gram_all[:, MODES:], HIGHEST), 0.0)
        project_t = project.T
        own = jnp.where(chosen, identity, 0.0)
        remainder = (
            jnp.concatenate([jnp.zeros((MODES, MODES), F32), own], 1)
            - dot_nn(project_t, coeff, HIGHEST)
        )
        gram = dot_nt(dot_nn(remainder, gram_all, HIGHEST), remainder, HIGHEST)
        low = batch * width
        tiles = inverse_factor(
            [gram[low + 8 * i : low + 8 * i + 8] for i in range(width // 8)], low
        )
        blank = jnp.zeros((width, MODES), F32)
        factor_inv = jnp.concatenate(
            [blank] * batch + tiles + [blank] * (batches - 1 - batch), 0
        )
        factor_t = dot_nn(factor_inv, gram, HIGHEST)
        factor_t = jnp.where((row <= lane) & chosen, factor_t, 0.0)
        fresh = dot_nn(factor_inv, remainder, HIGHEST)
        right = jnp.concatenate([project, factor_t], 0)
        right_t = jnp.concatenate([project_t, factor_t.T], 1)
        square_row = jnp.concatenate([squares, jnp.zeros((1, MODES), F32)], 1)
        frame[...] = jnp.concatenate([identity, jnp.zeros((MODES, MODES), F32)], 1)

        def sweep(repeat, carry):
            now = frame[...]
            grown = now * square_row + dot_nn(dot_nn(now, right, HIGHEST), right_t, HIGHEST)
            square = dot_nt(grown, grown, HIGHEST)
            inverse = inverse_factor([square[8 * i : 8 * i + 8] for i in range(MODES // 8)], 0)
            frame[...] = dot_nn(jnp.concatenate(inverse, 0), grown, HIGHEST)
            return carry

        lax.fori_loop(0, SWEEPS, sweep, 0)
        now = frame[...]
        side = dot_nn(now, right, HIGHEST)
        head = now[:, :MODES]
        energy = head * head * squares + side * side
        squares = dot_nt(jnp.ones((8, MODES), F32), energy, HIGHEST)[:1]
        coeff = dot_nn(now, jnp.concatenate([coeff, fresh], 0), HIGHEST)
    lead = coeff.astype(BF16)
    rest = (coeff - lead.astype(F32)).astype(BF16)
    coeff_ref[...] = jnp.concatenate([lead, rest], 0)
    out_ref[...] = jnp.sqrt(squares)


def apply_kernel(info_ref, coeff_ref, basis_ref, snap_ref, out_ref):
    lead, rest = load_split(pl.program_id(0), info_ref[0], basis_ref, snap_ref)
    both = dot_nn(coeff_ref[...], lead)
    out_ref[...] = (both[:MODES] + both[MODES:]) + dot_nn(coeff_ref[:MODES, :], rest)


def exchange(array, axis, move):
    size = lax.axis_size(axis)
    return lax.ppermute(array, axis, [(i, move(i)) for i in range(size)])


def ring_step(axis, stride, hop):
    def move(i):
        place = (i // stride) % 4
        return i + ((place + hop) % 4 - place) * stride

    return functools.partial(exchange, axis=axis, move=move)


def total_over_devices(mine, other):
    part = mine + exchange(other, "grp", lambda i: i ^ 1)
    for axis, stride in (("grp", 2), ("dev", 1), ("dev", 4)):
        part = (part + ring_step(axis, stride, 2)(part)) + (
            ring_step(axis, stride, 1)(part) + ring_step(axis, stride, 3)(part)
        )
    return part, exchange(part, "grp", lambda i: i ^ 1)


def per_device(basis_old, values_old, snapshots, wet_counts):
    batches, batch_width, cells = snapshots.shape
    snaps = snapshots.reshape(batches * batch_width, cells)
    parity = (lax.axis_index("grp") % 2).astype(jnp.int32)
    info = jnp.stack([wet_counts[0], parity])
    smem = pl.BlockSpec(memory_space=pltpu.SMEM)
    grid = (cells // CHUNK,)
    stream = pl.BlockSpec((MODES, CHUNK), lambda i: (0, i))
    half = jax.ShapeDtypeStruct((MODES + 8, MODES), F32)
    whole = pl.BlockSpec((MODES + 8, MODES), lambda i: (0, 0))
    mine, other = pl.pallas_call(
        gram_kernel,
        grid=grid,
        in_specs=[smem, stream, stream],
        out_specs=[whole, whole],
        out_shape=[half, half],
        scratch_shapes=[pltpu.VMEM((2 * MODES, 2 * MODES), F32)] * 2,
        name="gram",
    )(info, basis_old, snaps)
    mine, other = total_over_devices(mine, other)
    coeff, values = pl.pallas_call(
        functools.partial(core_kernel, batches),
        in_specs=[smem] + [pl.BlockSpec(memory_space=pltpu.VMEM)] * 3,
        out_specs=[pl.BlockSpec(memory_space=pltpu.VMEM)] * 2,
        out_shape=[
            jax.ShapeDtypeStruct((2 * MODES, 2 * MODES), BF16),
            jax.ShapeDtypeStruct((1, MODES), F32),
        ],
        scratch_shapes=[
            pltpu.VMEM((MODES, 2 * MODES), F32),
            pltpu.VMEM((MODES, MODES), F32),
        ],
        name="core",
    )(parity[None], mine, other, values_old[None, :])
    basis = pl.pallas_call(
        apply_kernel,
        grid=grid,
        in_specs=[smem, pl.BlockSpec((2 * MODES, 2 * MODES), lambda i: (0, 0)), stream, stream],
        out_specs=stream,
        out_shape=jax.ShapeDtypeStruct((MODES, cells), F32),
        name="apply",
    )(info, coeff, basis_old, snaps)
    return basis, values[0]


def solution(mesh):
    return jax.shard_map(
        per_device,
        mesh=mesh,
        in_specs=(P(None, ("grp", "dev")), P(), P(None, None, ("grp", "dev")), P(("grp", "dev"))),
        out_specs=(P(None, ("grp", "dev")), P()),
        check_vma=False,
    )
```

time: 611 us -> 107 us (0.18)
  blocking collectives: 324 us -> 0 us
  other arithmetic: 166 us -> 1.6 us
  matrix products: 86 us -> 0 us
  Pallas kernels: 0 us -> 70.3 us
  local copies, waits for them, and re-layouts: 27.7 us -> 0.63 us
  starting transfers between devices: 0 us -> 20 us
  waiting for transfers between devices: 0 us -> 13.2 us
    psum x4 -> x0, blocking collectives: 255 us -> none  [the longest x2 129 us: update_one(): gram = lax.psum(matmul_nt(remainder, remainder), ('grp', 'dev')) / wet_total]
    another operation x40 -> x1, other arithmetic: 162 us -> 0.65 us  [per_device(): info = jnp.stack([wet_counts[0], parity])]
    dot_general x28 -> x0, matrix products: 72.6 us -> none  [the longest x18 46.3 us: matmul_tn(): lax.dot_general(left_op, right_op, (((0,), (0,)), ((), ())), precision=la...]
    pallas_call x0 -> x3, Pallas kernels: none -> 70.3 us  [the longest x1 45.1 us: per_device(): pl.pallas_call(functools.partial(core_kernel, batches), in_specs=[smem] +...]
    unnamed x1 -> x0, blocking collectives: 68.6 us -> none
    ppermute x0 -> x11, starting transfers between devices: none -> 20 us  [exchange(): return lax.ppermute(array, axis, [(i, move(i)) for i in range(size)])]
    while x16 -> x0, local copies, waits for them, and re-layouts: 18.6 us -> none
    another operation x8 -> x0, matrix products: 13.4 us -> none  [the longest x2 11.5 us: update_one(): jax.scipy.linalg.solve_triangular(factor, remainder, lower=True)]
  transfers between devices with their start and end apart: 0 -> 11, of which waited for: 0 -> 6; matrix products, arithmetic and copies ran while one was open for 0% -> 0% of each run, Pallas kernels for 0% -> 0%
where the time goes in v1:
time: 107 us
  Pallas kernels  70.3 us (66%)
  starting transfers between devices  20 us (19%)
  waiting for transfers between devices  13.2 us (12%)
  other arithmetic  1.6 us (1%)
  between operations  1.32 us (1%)
    pallas_call x1, Pallas kernels, per_device(): pl.pallas_call(functools.partial(core_kernel, batches), in_specs=[smem] +...  45.1 us
    ppermute x11, starting transfers between devices, exchange(): return lax.ppermute(array, axis, [(i, move(i)) for i in range(size)])  20 us
    ppermute x11, waiting for transfers between devices, exchange(): return lax.ppermute(array, axis, [(i, move(i)) for i in range(size)])  13.2 us
    pallas_call x1, Pallas kernels, per_device(): pl.pallas_call(apply_kernel, grid=grid, in_specs=[smem, pl.BlockSpec((2 *...  12.7 us
    pallas_call x1, Pallas kernels, per_device(): pl.pallas_call(gram_kernel, grid=grid, in_specs=[smem, stream, stream], o...  12.5 us
  transfers between devices with their start and end apart: 11, of which 6 were waited for; matrix products, arithmetic and copies ran while one was open for 0% of the time, Pallas kernels for 0%

profile of v1, /device:TPU:1, one launch (start us, length us, event | category | flops | bytes accessed | tf_op | source)
XLA Modules:
  0.0 107.0 jit_solution(7893834405064096311)
XLA Ops:
  1.3 0.6 pad_add_fusion.info_ref
  1.9 12.5 %gram.1 = (f32[136,128]{1,0:T(8,128)}, f32[136,128]{1,0:T(8,128)}) custom-call(s32[2]{0:T(128)} %pad_add_fusion.info_ref, f32[128,16384]{1,0:T(8,128)} %basis_ref.3, f32[128,16384]{1,0:T(8,128)} %bitcast.4), custom_call_target="tpu_custom_call" | custom-call | tf_op jit(solution)/shard_map/gram/pallas_call | solution.py:248
  14.4 1.4 %collective-permute-start = (f32[136,128]{1,0:T(8,128)}, f32[136,128]{1,0:T(8,128)S(1)}, u32[]{:S(2)}, u32[]{:S(2)}) collective-permute-start(f32[136,128]{1,0:T(8,128)} %get-tuple-element.7), channel_id=1, source_target_pairs={{0,16},{16,0},{32,48},{48,32},{64,80},{80,64},{96,112},{112,96},{1... | collective-permute-start | bytes 208904 | tf_op jit(solution)/shard_map/ppermute | solution.py:218
  15.8 1.1 %collective-permute-done = f32[136,128]{1,0:T(8,128)S(1)} collective-permute-done((f32[136,128]{1,0:T(8,128)}, f32[136,128]{1,0:T(8,128)S(1)}, u32[]{:S(2)}, u32[]{:S(2)}) %collective-permute-start) | collective-permute-done | bytes 69664 | tf_op jit(solution)/shard_map/ppermute | solution.py:218
  16.9 0.9 add.35
  17.8 2.9 %collective-permute-start.3 = (f32[136,128]{1,0:T(8,128)S(1)}, f32[136,128]{1,0:T(8,128)S(1)}, u32[]{:S(2)}, u32[]{:S(2)}) collective-permute-start(f32[136,128]{1,0:T(8,128)S(1)} %add.35), channel_id=1, source_target_pairs={{0,96},{16,112},{32,0},{48,16},{64,32},{80,48},{96,64},{112,80},{1... | collective-permute-start | bytes 208904 | tf_op jit(solution)/shard_map/ppermute | solution.py:218
  20.8 0.0 collective-permute-start.2
  20.8 1.6 %collective-permute-start.1 = (f32[136,128]{1,0:T(8,128)S(1)}, f32[136,128]{1,0:T(8,128)S(1)}, u32[]{:S(2)}, u32[]{:S(2)}) collective-permute-start(f32[136,128]{1,0:T(8,128)S(1)} %add.35), channel_id=1, source_target_pairs={{0,64},{16,80},{32,96},{48,112},{64,0},{80,16},{96,32},{112,48},{1... | collective-permute-start | bytes 208904 | tf_op jit(solution)/shard_map/ppermute | solution.py:218
  22.4 0.0 collective-permute-done.3
  22.4 3.6 %collective-permute-done.2 = f32[136,128]{1,0:T(8,128)S(1)} collective-permute-done((f32[136,128]{1,0:T(8,128)S(1)}, f32[136,128]{1,0:T(8,128)S(1)}, u32[]{:S(2)}, u32[]{:S(2)}) %collective-permute-start.2) | collective-permute-done | bytes 69664 | tf_op jit(solution)/shard_map/ppermute | solution.py:218
  26.0 0.4 collective-permute-done.1
  26.4 2.5 %collective-permute-start.6 = (f32[136,128]{1,0:T(8,128)S(1)}, f32[136,128]{1,0:T(8,128)S(1)}, u32[]{:S(2)}, u32[]{:S(2)}) collective-permute-start(f32[136,128]{1,0:T(8,128)S(1)} %add_add_fusion.2), channel_id=1, source_target_pairs={{0,3},{1,0},{2,1},{3,2},{4,7},{5,4},{6,5},{7,6},{8,11},{9,8},{10,9... | collective-permute-start | bytes 208904 | tf_op jit(solution)/shard_map/ppermute | solution.py:218
  29.0 0.0 collective-permute-start.5
  29.0 1.7 %collective-permute-start.4 = (f32[136,128]{1,0:T(8,128)S(1)}, f32[136,128]{1,0:T(8,128)S(1)}, u32[]{:S(2)}, u32[]{:S(2)}) collective-permute-start(f32[136,128]{1,0:T(8,128)S(1)} %add_add_fusion.2), channel_id=1, source_target_pairs={{0,2},{1,3},{2,0},{3,1},{4,6},{5,7},{6,4},{7,5},{8,10},{9,11},{10,... | collective-permute-start | bytes 208904 | tf_op jit(solution)/shard_map/ppermute | solution.py:218
  30.7 0.0 collective-permute-done.6
  30.7 3.4 %collective-permute-done.5 = f32[136,128]{1,0:T(8,128)S(1)} collective-permute-done((f32[136,128]{1,0:T(8,128)S(1)}, f32[136,128]{1,0:T(8,128)S(1)}, u32[]{:S(2)}, u32[]{:S(2)}) %collective-permute-start.5) | collective-permute-done | bytes 69664 | tf_op jit(solution)/shard_map/ppermute | solution.py:218
  34.1 0.0 collective-permute-done.4
  34.1 3.8 %collective-permute-start.9 = (f32[136,128]{1,0:T(8,128)S(1)}, f32[136,128]{1,0:T(8,128)S(1)}, u32[]{:S(2)}, u32[]{:S(2)}) collective-permute-start(f32[136,128]{1,0:T(8,128)S(1)} %add_add_fusion.1), channel_id=1, source_target_pairs={{0,12},{1,13},{2,14},{3,15},{4,0},{5,1},{6,2},{7,3},{8,4},{9,5},{1... | collective-permute-start | bytes 208904 | tf_op jit(solution)/shard_map/ppermute | solution.py:218
  37.9 0.0 collective-permute-start.8
  37.9 1.3 %collective-permute-start.7 = (f32[136,128]{1,0:T(8,128)S(1)}, f32[136,128]{1,0:T(8,128)S(1)}, u32[]{:S(2)}, u32[]{:S(2)}) collective-permute-start(f32[136,128]{1,0:T(8,128)S(1)} %add_add_fusion.1), channel_id=1, source_target_pairs={{0,8},{1,9},{2,10},{3,11},{4,12},{5,13},{6,14},{7,15},{8,0},{9,1},... | collective-permute-start | bytes 208904 | tf_op jit(solution)/shard_map/ppermute | solution.py:218
  39.2 0.0 collective-permute-done.9
  39.3 3.7 %collective-permute-done.8 = f32[136,128]{1,0:T(8,128)S(1)} collective-permute-done((f32[136,128]{1,0:T(8,128)S(1)}, f32[136,128]{1,0:T(8,128)S(1)}, u32[]{:S(2)}, u32[]{:S(2)}) %collective-permute-start.8) | collective-permute-done | bytes 69664 | tf_op jit(solution)/shard_map/ppermute | solution.py:218
  43.0 0.0 collective-permute-done.7
  43.1 0.0 copy-start
  43.1 4.6 %collective-permute-start.10 = (f32[136,128]{1,0:T(8,128)S(1)}, f32[136,128]{1,0:T(8,128)S(1)}, u32[]{:S(2)}, u32[]{:S(2)}) collective-permute-start(f32[136,128]{1,0:T(8,128)S(1)} %add_add_fusion.mine_ref), channel_id=1, source_target_pairs={{0,16},{16,0},{32,48},{48,32},{64,80},{80,64},{96,112},{112,96},{1... | collective-permute-start | bytes 208904 | tf_op jit(solution)/shard_map/ppermute | solution.py:218
  47.7 0.9 collective-permute-done.10.other_ref
  48.6 0.0 copy-start.1
  48.6 0.0 copy-done
  48.6 0.6 copy-done.1
  49.2 45.1 %core.1 = (bf16[256,256]{1,0:T(8,128)(2,1)}, f32[1,128]{1,0:T(1,128)}) custom-call(s32[1]{0:T(128)} %bitcast.parity_ref, f32[136,128]{1,0:T(8,128)} %copy-done, f32[136,128]{1,0:T(8,128)} %copy-done.1, f32[1,128]{1,0:T(1,128)} %bitcast.6), custom_call_target="tpu_custom_call" | custom-call | tf_op jit(solution)/shard_map/core/pallas_call | solution.py:258
  94.3 12.7 %apply.1 = f32[128,16384]{1,0:T(8,128)} custom-call(s32[2]{0:T(128)} %pad_add_fusion.info_ref, bf16[256,256]{1,0:T(8,128)(2,1)} %get-tuple-element.8.coeff_ref, f32[128,16384]{1,0:T(8,128)} %basis_ref.3, f32[128,16384]{1,0:T(8,128)} %bitcast.5), custom_call_target="tpu_custom_call" | custom-call | tf_op jit(solution)/shard_map/apply/pallas_call | solution.py:272
  (3 shorter events, 0.1 us)
Async XLA Ops:
  14.4 2.5 %collective-permute-start = (f32[136,128]{1,0:T(8,128)}, f32[136,128]{1,0:T(8,128)S(1)}, u32[]{:S(2)}, u32[]{:S(2)}) collective-permute-start(f32[136,128]{1,0:T(8,128)} %get-tuple-element.7), channel_id=1, source_target_pairs={{0,16},{16,0},{32,48},{48,32},{64,80},{80,64},{96,112},{112,96},{1... | collective-permute-start | bytes 208904 | tf_op jit(solution)/shard_map/ppermute | solution.py:218
  17.8 4.6 %collective-permute-start.3 = (f32[136,128]{1,0:T(8,128)S(1)}, f32[136,128]{1,0:T(8,128)S(1)}, u32[]{:S(2)}, u32[]{:S(2)}) collective-permute-start(f32[136,128]{1,0:T(8,128)S(1)} %add.35), channel_id=1, source_target_pairs={{0,96},{16,112},{32,0},{48,16},{64,32},{80,48},{96,64},{112,80},{1... | collective-permute-start | bytes 208904 | tf_op jit(solution)/shard_map/ppermute | solution.py:218
  20.8 5.2 %collective-permute-start.2 = (f32[136,128]{1,0:T(8,128)S(1)}, f32[136,128]{1,0:T(8,128)S(1)}, u32[]{:S(2)}, u32[]{:S(2)}) collective-permute-start(f32[136,128]{1,0:T(8,128)S(1)} %add.35), channel_id=1, source_target_pairs={{0,32},{16,48},{32,64},{48,80},{64,96},{80,112},{96,0},{112,16},{1... | collective-permute-start | bytes 208904 | tf_op jit(solution)/shard_map/ppermute | solution.py:218
  20.8 5.6 %collective-permute-start.1 = (f32[136,128]{1,0:T(8,128)S(1)}, f32[136,128]{1,0:T(8,128)S(1)}, u32[]{:S(2)}, u32[]{:S(2)}) collective-permute-start(f32[136,128]{1,0:T(8,128)S(1)} %add.35), channel_id=1, source_target_pairs={{0,64},{16,80},{32,96},{48,112},{64,0},{80,16},{96,32},{112,48},{1... | collective-permute-start | bytes 208904 | tf_op jit(solution)/shard_map/ppermute | solution.py:218
  26.4 4.3 %collective-permute-start.6 = (f32[136,128]{1,0:T(8,128)S(1)}, f32[136,128]{1,0:T(8,128)S(1)}, u32[]{:S(2)}, u32[]{:S(2)}) collective-permute-start(f32[136,128]{1,0:T(8,128)S(1)} %add_add_fusion.2), channel_id=1, source_target_pairs={{0,3},{1,0},{2,1},{3,2},{4,7},{5,4},{6,5},{7,6},{8,11},{9,8},{10,9... | collective-permute-start | bytes 208904 | tf_op jit(solution)/shard_map/ppermute | solution.py:218
  29.0 5.1 %collective-permute-start.5 = (f32[136,128]{1,0:T(8,128)S(1)}, f32[136,128]{1,0:T(8,128)S(1)}, u32[]{:S(2)}, u32[]{:S(2)}) collective-permute-start(f32[136,128]{1,0:T(8,128)S(1)} %add_add_fusion.2), channel_id=1, source_target_pairs={{0,1},{1,2},{2,3},{3,0},{4,5},{5,6},{6,7},{7,4},{8,9},{9,10},{10,1... | collective-permute-start | bytes 208904 | tf_op jit(solution)/shard_map/ppermute | solution.py:218
  29.0 5.1 %collective-permute-start.4 = (f32[136,128]{1,0:T(8,128)S(1)}, f32[136,128]{1,0:T(8,128)S(1)}, u32[]{:S(2)}, u32[]{:S(2)}) collective-permute-start(f32[136,128]{1,0:T(8,128)S(1)} %add_add_fusion.2), channel_id=1, source_target_pairs={{0,2},{1,3},{2,0},{3,1},{4,6},{5,7},{6,4},{7,5},{8,10},{9,11},{10,... | collective-permute-start | bytes 208904 | tf_op jit(solution)/shard_map/ppermute | solution.py:218
  34.1 5.2 %collective-permute-start.9 = (f32[136,128]{1,0:T(8,128)S(1)}, f32[136,128]{1,0:T(8,128)S(1)}, u32[]{:S(2)}, u32[]{:S(2)}) collective-permute-start(f32[136,128]{1,0:T(8,128)S(1)} %add_add_fusion.1), channel_id=1, source_target_pairs={{0,12},{1,13},{2,14},{3,15},{4,0},{5,1},{6,2},{7,3},{8,4},{9,5},{1... | collective-permute-start | bytes 208904 | tf_op jit(solution)/shard_map/ppermute | solution.py:218
  37.9 5.1 %collective-permute-start.8 = (f32[136,128]{1,0:T(8,128)S(1)}, f32[136,128]{1,0:T(8,128)S(1)}, u32[]{:S(2)}, u32[]{:S(2)}) collective-permute-start(f32[136,128]{1,0:T(8,128)S(1)} %add_add_fusion.1), channel_id=1, source_target_pairs={{0,4},{1,5},{2,6},{3,7},{4,8},{5,9},{6,10},{7,11},{8,12},{9,13},{1... | collective-permute-start | bytes 208904 | tf_op jit(solution)/shard_map/ppermute | solution.py:218
  37.9 5.1 %collective-permute-start.7 = (f32[136,128]{1,0:T(8,128)S(1)}, f32[136,128]{1,0:T(8,128)S(1)}, u32[]{:S(2)}, u32[]{:S(2)}) collective-permute-start(f32[136,128]{1,0:T(8,128)S(1)} %add_add_fusion.1), channel_id=1, source_target_pairs={{0,8},{1,9},{2,10},{3,11},{4,12},{5,13},{6,14},{7,15},{8,0},{9,1},... | collective-permute-start | bytes 208904 | tf_op jit(solution)/shard_map/ppermute | solution.py:218
  43.1 5.5 %copy-start = (f32[136,128]{1,0:T(8,128)}, f32[136,128]{1,0:T(8,128)S(1)}, u32[]{:S(2)}) copy-start(f32[136,128]{1,0:T(8,128)S(1)} %add_add_fusion.mine_ref) | copy-start | bytes 208900
  43.1 5.5 %collective-permute-start.10 = (f32[136,128]{1,0:T(8,128)S(1)}, f32[136,128]{1,0:T(8,128)S(1)}, u32[]{:S(2)}, u32[]{:S(2)}) collective-permute-start(f32[136,128]{1,0:T(8,128)S(1)} %add_add_fusion.mine_ref), channel_id=1, source_target_pairs={{0,16},{16,0},{32,48},{48,32},{64,80},{80,64},{96,112},{112,96},{1... | collective-permute-start | bytes 208904 | tf_op jit(solution)/shard_map/ppermute | solution.py:218
  48.6 0.6 copy-start.1

commit v2 on v1

--- a/solution.py
+++ b/solution.py
@@ -10,7 +10,11 @@
 BLOCK = 128
 SWEEPS = 3
 MODES = 128
-CHUNK = 2048
+GRAM_PARTS = 8
+APPLY_PARTS = 16
+GRAM_VMEM = 8 << 20
+CORE_VMEM = 8 << 20
+APPLY_VMEM = 14 << 20
 F32 = jnp.float32
 BF16 = jnp.bfloat16
 HIGHEST = lax.Precision.HIGHEST
@@ -28,48 +32,69 @@
     )
 
 
-def load_split(step, wet, basis_ref, snap_ref):
-    width = basis_ref.shape[1]
-    cell = lax.broadcasted_iota(jnp.int32, snap_ref.shape, 1) + step * width
-    columns = jnp.where(cell < wet * BLOCK, snap_ref[...], 0.0)
-    rows = jnp.concatenate([basis_ref[...], columns], 0)
-    lead = rows.astype(BF16)
-    rest = (rows - lead.astype(F32)).astype(BF16)
-    return lead, rest
-
-
-def gram_kernel(info_ref, basis_ref, snap_ref, mine_ref, other_ref, even_acc, cross_acc):
-    step = pl.program_id(0)
-
-    @pl.when(step == 0)
-    def _():
-        even_acc[...] = jnp.zeros_like(even_acc)
-        cross_acc[...] = jnp.zeros_like(cross_acc)
-
-    lead, rest = load_split(step, info_ref[0], basis_ref, snap_ref)
-    even_acc[...] += dot_nt(lead, lead) + dot_nt(rest, rest)
-    cross_acc[...] += dot_nt(lead, rest)
-
-    @pl.when(step == pl.num_programs(0) - 1)
-    def _():
-        cross = cross_acc[...]
-        gram = even_acc[...] + (cross + cross.T)
-        row = lax.broadcasted_iota(jnp.int32, (MODES, MODES), 0)
-        lane = lax.broadcasted_iota(jnp.int32, (MODES, MODES), 1)
-        snap_gram = gram[MODES:, MODES:]
-        diagonal = jnp.sum(jnp.where(row == lane, snap_gram, 0.0), 0, keepdims=True)
-        extra = jnp.where(
-            lax.broadcasted_iota(jnp.int32, (8, MODES), 0) == 0,
-            jnp.broadcast_to(diagonal, (8, MODES)),
-            jnp.full((8, MODES), info_ref[0].astype(F32)),
-        )
-        symmetric = jnp.concatenate(
-            [jnp.where(lane <= row, gram[:MODES, :MODES], snap_gram), extra], 0
-        )
-        mixed = jnp.concatenate([gram[:MODES, MODES:], jnp.zeros((8, MODES), F32)], 0)
-        first = info_ref[1] == 0
-        mine_ref[...] = jnp.where(first, symmetric, mixed)
-        other_ref[...] = jnp.where(first, mixed, symmetric)
+def split_rows(basis, snap, start, wet):
+    cell = lax.broadcasted_iota(jnp.int32, snap.shape, 1) + start
+    snap = jnp.where(cell < wet * BLOCK, snap, 0.0)
+    basis_lead, snap_lead = basis.astype(BF16), snap.astype(BF16)
+    basis_rest = (basis - basis_lead.astype(F32)).astype(BF16)
+    snap_rest = (snap - snap_lead.astype(F32)).astype(BF16)
+    return (
+        jnp.concatenate([basis_lead, snap_lead], 0),
+        jnp.concatenate([basis_rest, snap_rest], 0),
+    )
+
+
+def gram_kernel(
+    info_ref, basis_hbm, snap_hbm, mine_ref, other_ref, basis_buf, snap_buf, arrived, even_acc, cross_acc, energy
+):
+    width = basis_hbm.shape[1] // GRAM_PARTS
+    copies = []
+    for part in range(GRAM_PARTS):
+        span = pl.ds(part * width, width)
+        copies.append(
+            [
+                pltpu.make_async_copy(source.at[:, span], target.at[:, span], arrived.at[which, part])
+                for which, (source, target) in enumerate(
+                    [(basis_hbm, basis_buf), (snap_hbm, snap_buf)]
+                )
+            ]
+        )
+        for copy in copies[-1]:
+            copy.start()
+    for part in range(GRAM_PARTS):
+        for copy in copies[part]:
+            copy.wait()
+        span = pl.ds(part * width, width)
+        lead, rest = split_rows(basis_buf[:, span], snap_buf[:, span], part * width, info_ref[0])
+        step, mixed_step = dot_nt(lead, lead), dot_nt(rest, lead)
+        square = rest.astype(F32)
+        square = square * square
+        folded = square[:, :BLOCK]
+        for k in range(1, width // BLOCK):
+            folded = folded + square[:, k * BLOCK : (k + 1) * BLOCK]
+        even_acc[...] = step if part == 0 else even_acc[...] + step
+        cross_acc[...] = mixed_step if part == 0 else cross_acc[...] + mixed_step
+        energy[...] = folded if part == 0 else energy[...] + folded
+
+    row = lax.broadcasted_iota(jnp.int32, (MODES, MODES), 0)
+    lane = lax.broadcasted_iota(jnp.int32, (MODES, MODES), 1)
+    cross = cross_acc[...]
+    gram = even_acc[...] + (cross + cross.T)
+    extra_basis = jnp.sum(energy[:MODES, :], 1, keepdims=True)
+    extra_snap = jnp.sum(energy[MODES:, :], 1, keepdims=True)
+    basis_gram = gram[:MODES, :MODES] + jnp.where(row == lane, extra_basis, 0.0)
+    snap_gram = gram[MODES:, MODES:]
+    diagonal = jnp.sum(jnp.where(row == lane, snap_gram + extra_snap, 0.0), 0, keepdims=True)
+    extra = jnp.where(
+        lax.broadcasted_iota(jnp.int32, (8, MODES), 0) == 0,
+        jnp.broadcast_to(diagonal, (8, MODES)),
+        jnp.full((8, MODES), info_ref[0].astype(F32)),
+    )
+    symmetric = jnp.concatenate([jnp.where(lane <= row, basis_gram, snap_gram), extra], 0)
+    mixed = jnp.concatenate([gram[:MODES, MODES:], jnp.zeros((8, MODES), F32)], 0)
+    first = info_ref[1] == 0
+    mine_ref[...] = jnp.where(first, symmetric, mixed)
+    other_ref[...] = jnp.where(first, mixed, symmetric)
 
 
 def lane_of(tile, index):
@@ -131,7 +156,7 @@
     return finished
 
 
-def core_kernel(batches, parity_ref, mine_ref, other_ref, values_ref, coeff_ref, out_ref, frame, gram_buf):
+def core_kernel(batches, parity_ref, mine_ref, other_ref, values_ref, coeff_ref, out_ref, frame, grown_buf):
     first = parity_ref[0] == 0
     mine, other = mine_ref[...], other_ref[...]
     symmetric = jnp.where(first, mine, other)
@@ -207,10 +232,20 @@
     out_ref[...] = jnp.sqrt(squares)
 
 
-def apply_kernel(info_ref, coeff_ref, basis_ref, snap_ref, out_ref):
-    lead, rest = load_split(pl.program_id(0), info_ref[0], basis_ref, snap_ref)
-    both = dot_nn(coeff_ref[...], lead)
-    out_ref[...] = (both[:MODES] + both[MODES:]) + dot_nn(coeff_ref[:MODES, :], rest)
+def apply_kernel(info_ref, coeff_ref, basis_ref, snap_ref, out_hbm, buffer, sent):
+    width = out_hbm.shape[1] // APPLY_PARTS
+    copies = []
+    for part in range(APPLY_PARTS):
+        span = pl.ds(part * width, width)
+        lead, rest = split_rows(basis_ref[:, span], snap_ref[:, span], part * width, info_ref[0])
+        both = dot_nn(coeff_ref[...], lead)
+        buffer[:, span] = (both[:MODES] + both[MODES:]) + dot_nn(coeff_ref[:MODES, :], rest)
+        copies.append(
+            pltpu.make_async_copy(buffer.at[:, span], out_hbm.at[:, span], sent.at[part])
+        )
+        copies[-1].start()
+    for copy in copies:
+        copy.wait()
 
 
 def exchange(array, axis, move):
@@ -235,48 +270,73 @@
     return part, exchange(part, "grp", lambda i: i ^ 1)
 
 
+VMEM = pl.BlockSpec(memory_space=pltpu.VMEM)
+SMEM = pl.BlockSpec(memory_space=pltpu.SMEM)
+ANYWHERE = pl.BlockSpec(memory_space=pl.ANY)
+
+
+def gram_call(info, basis, snaps):
+    cells = basis.shape[1]
+    half = jax.ShapeDtypeStruct((MODES + 8, MODES), F32)
+    near = jax.ShapeDtypeStruct((MODES, cells), F32)
+    return pl.pallas_call(
+        gram_kernel,
+        in_specs=[SMEM, ANYWHERE, ANYWHERE],
+        out_specs=[VMEM] * 4,
+        out_shape=[half, half, near, near],
+        scratch_shapes=[
+            pltpu.SemaphoreType.DMA((2, GRAM_PARTS)),
+            pltpu.VMEM((2 * MODES, 2 * MODES), F32),
+            pltpu.VMEM((2 * MODES, 2 * MODES), F32),
+            pltpu.VMEM((2 * MODES, BLOCK), F32),
+        ],
+        compiler_params=pltpu.CompilerParams(vmem_limit_bytes=GRAM_VMEM),
+        name="gram",
+    )(info, basis, snaps)
+
+
+def core_call(parity, mine, other, values, batches=2):
+    return pl.pallas_call(
+        functools.partial(core_kernel, batches),
+        in_specs=[SMEM, VMEM, VMEM, VMEM],
+        out_specs=[VMEM, VMEM],
+        out_shape=[
+            jax.ShapeDtypeStruct((2 * MODES, 2 * MODES), BF16),
+            jax.ShapeDtypeStruct((1, MODES), F32),
+        ],
+        scratch_shapes=[pltpu.VMEM((MODES, 2 * MODES), F32)] * 2,
+        compiler_params=pltpu.CompilerParams(vmem_limit_bytes=CORE_VMEM),
+        name="core",
+    )(parity, mine, other, values)
+
+
+def apply_call(info, coeff, basis, snaps):
+    cells = basis.shape[1]
+    return pl.pallas_call(
+        apply_kernel,
+        in_specs=[SMEM, VMEM, VMEM, VMEM],
+        out_specs=ANYWHERE,
+        out_shape=jax.ShapeDtypeStruct((MODES, cells), F32),
+        scratch_shapes=[
+            pltpu.VMEM((MODES, cells), F32),
+            pltpu.SemaphoreType.DMA((APPLY_PARTS,)),
+        ],
+        compiler_params=pltpu.CompilerParams(vmem_limit_bytes=APPLY_VMEM),
+        name="apply",
+    )(info, coeff, basis, snaps)
+
+
 def per_device(basis_old, values_old, snapshots, wet_counts):
     batches, batch_width, cells = snapshots.shape
     snaps = snapshots.reshape(batches * batch_width, cells)
     parity = (lax.axis_index("grp") % 2).astype(jnp.int32)
     info = jnp.stack([wet_counts[0], parity])
-    smem = pl.BlockSpec(memory_space=pltpu.SMEM)
-    grid = (cells // CHUNK,)
-    stream = pl.BlockSpec((MODES, CHUNK), lambda i: (0, i))
-    half = jax.ShapeDtypeStruct((MODES + 8, MODES), F32)
-    whole = pl.BlockSpec((MODES + 8, MODES), lambda i: (0, 0))
-    mine, other = pl.pallas_call(
-        gram_kernel,
-        grid=grid,
-        in_specs=[smem, stream, stream],
-        out_specs=[whole, whole],
-        out_shape=[half, half],
-        scratch_shapes=[pltpu.VMEM((2 * MODES, 2 * MODES), F32)] * 2,
-        name="gram",
-    )(info, basis_old, snaps)
+    far = pltpu.with_memory_space_constraint(basis_old, pltpu.HBM)
+    far_snaps = pltpu.with_memory_space_constraint(snaps, pltpu.HBM)
+    mine, other, near_basis, near_snaps = gram_call(info, far, far_snaps)
     mine, other = total_over_devices(mine, other)
-    coeff, values = pl.pallas_call(
-        functools.partial(core_kernel, batches),
-        in_specs=[smem] + [pl.BlockSpec(memory_space=pltpu.VMEM)] * 3,
-        out_specs=[pl.BlockSpec(memory_space=pltpu.VMEM)] * 2,
-        out_shape=[
-            jax.ShapeDtypeStruct((2 * MODES, 2 * MODES), BF16),
-            jax.ShapeDtypeStruct((1, MODES), F32),
-        ],
-        scratch_shapes=[
-            pltpu.VMEM((MODES, 2 * MODES), F32),
-            pltpu.VMEM((MODES, MODES), F32),
-        ],
-        name="core",
-    )(parity[None], mine, other, values_old[None, :])
-    basis = pl.pallas_call(
-        apply_kernel,
-        grid=grid,
-        in_specs=[smem, pl.BlockSpec((2 * MODES, 2 * MODES), lambda i: (0, 0)), stream, stream],
-        out_specs=stream,
-        out_shape=jax.ShapeDtypeStruct((MODES, cells), F32),
-        name="apply",
-    )(info, coeff, basis_old, snaps)
+    coeff, values = core_call(parity[None], mine, other, values_old[None, :], batches)
+    basis = apply_call(info, coeff, near_basis, near_snaps)
     return basis, values[0]
 
 

time: 107 us -> 93 us (0.87)
  Pallas kernels: 70.3 us -> 58 us
  other arithmetic: 1.6 us -> 0.13 us
    pallas_call x3, Pallas kernels: 70.3 us -> 58 us  [the longest x1 44.2 us: core_call(): pl.pallas_call(functools.partial(core_kernel, batches), in_specs=[SMEM, V...]
  transfers between devices with their start and end apart: 11 -> 11, of which waited for: 6 -> 7; matrix products, arithmetic and copies ran while one was open for 0% -> 0% of each run, Pallas kernels for 0% -> 0%
where the time goes in v2:
time: 93 us; the launch traced here: 92.9 us
  Pallas kernels  58 us (62%)
  starting transfers between devices  20.2 us (22%)
  waiting for transfers between devices  13 us (14%)
  between operations  1.5 us (2%)
    pallas_call x1, Pallas kernels, core_call(): pl.pallas_call(functools.partial(core_kernel, batches), in_specs=[SMEM, V...  44.2 us
    ppermute x11, starting transfers between devices, exchange(): return lax.ppermute(array, axis, [(i, move(i)) for i in range(size)])  20.2 us
    ppermute x11, waiting for transfers between devices, exchange(): return lax.ppermute(array, axis, [(i, move(i)) for i in range(size)])  13 us
    pallas_call x1, Pallas kernels, gram_call(): pl.pallas_call(gram_kernel, in_specs=[SMEM, ANYWHERE, ANYWHERE], out_spec...  8.41 us
    pallas_call x1, Pallas kernels, apply_call(): pl.pallas_call(apply_kernel, in_specs=[SMEM, VMEM, VMEM, VMEM], out_specs...  5.4 us
  transfers between devices with their start and end apart: 11, of which 7 were waited for; matrix products, arithmetic and copies ran while one was open for 0% of the time, Pallas kernels for 0%

profile of v2, /device:TPU:1, one launch (start us, length us, event | category | flops | bytes accessed | tf_op | source)
XLA Modules:
  0.0 92.9 jit_solution(14167652702376565166)
XLA Ops:
  1.3 0.1 pad_add_fusion.info_ref
  1.4 0.0 copy-start
  1.4 8.4 %gram.1 = (f32[136,128]{1,0:T(8,128)S(1)}, f32[136,128]{1,0:T(8,128)S(1)}, f32[128,16384]{1,0:T(8,128)S(1)}, f32[128,16384]{1,0:T(8,128)S(1)}) custom-call(s32[2]{0:T(128)S(1)} %pad_add_fusion.info_ref, f32[128,16384]{1,0:T(8,128)} %basis_hbm.1, f32[128,16384]{1,0:T(8,128)} %bitcast.5), custom_call_target="tpu_custom_call" | custom-call | tf_op jit(solution)/shard_map/gram/pallas_call | solution.py:282
  9.8 1.5 %collective-permute-start = (f32[136,128]{1,0:T(8,128)S(1)}, f32[136,128]{1,0:T(8,128)S(1)}, u32[]{:S(2)}, u32[]{:S(2)}) collective-permute-start(f32[136,128]{1,0:T(8,128)S(1)} %get-tuple-element.9), channel_id=1, source_target_pairs={{0,16},{16,0},{32,48},{48,32},{64,80},{80,64},{96,112},{112,96},{1... | collective-permute-start | bytes 208904 | tf_op jit(solution)/shard_map/ppermute | solution.py:253
  11.3 0.9 collective-permute-done
  12.2 2.9 %collective-permute-start.3 = (f32[136,128]{1,0:T(8,128)S(1)}, f32[136,128]{1,0:T(8,128)S(1)}, u32[]{:S(2)}, u32[]{:S(2)}) collective-permute-start(f32[136,128]{1,0:T(8,128)S(1)} %add.35), channel_id=1, source_target_pairs={{0,96},{16,112},{32,0},{48,16},{64,32},{80,48},{96,64},{112,80},{1... | collective-permute-start | bytes 208904 | tf_op jit(solution)/shard_map/ppermute | solution.py:253
  15.1 0.0 collective-permute-start.2
  15.1 1.6 %collective-permute-start.1 = (f32[136,128]{1,0:T(8,128)S(1)}, f32[136,128]{1,0:T(8,128)S(1)}, u32[]{:S(2)}, u32[]{:S(2)}) collective-permute-start(f32[136,128]{1,0:T(8,128)S(1)} %add.35), channel_id=1, source_target_pairs={{0,64},{16,80},{32,96},{48,112},{64,0},{80,16},{96,32},{112,48},{1... | collective-permute-start | bytes 208904 | tf_op jit(solution)/shard_map/ppermute | solution.py:253
  16.7 0.0 collective-permute-done.3
  16.7 3.6 %collective-permute-done.2 = f32[136,128]{1,0:T(8,128)S(1)} collective-permute-done((f32[136,128]{1,0:T(8,128)S(1)}, f32[136,128]{1,0:T(8,128)S(1)}, u32[]{:S(2)}, u32[]{:S(2)}) %collective-permute-start.2) | collective-permute-done | bytes 69664 | tf_op jit(solution)/shard_map/ppermute | solution.py:253
  20.3 0.4 collective-permute-done.1
  20.7 2.5 %collective-permute-start.6 = (f32[136,128]{1,0:T(8,128)S(1)}, f32[136,128]{1,0:T(8,128)S(1)}, u32[]{:S(2)}, u32[]{:S(2)}) collective-permute-start(f32[136,128]{1,0:T(8,128)S(1)} %add_add_fusion.2), channel_id=1, source_target_pairs={{0,3},{1,0},{2,1},{3,2},{4,7},{5,4},{6,5},{7,6},{8,11},{9,8},{10,9... | collective-permute-start | bytes 208904 | tf_op jit(solution)/shard_map/ppermute | solution.py:253
  23.3 0.0 collective-permute-start.5
  23.3 1.7 %collective-permute-start.4 = (f32[136,128]{1,0:T(8,128)S(1)}, f32[136,128]{1,0:T(8,128)S(1)}, u32[]{:S(2)}, u32[]{:S(2)}) collective-permute-start(f32[136,128]{1,0:T(8,128)S(1)} %add_add_fusion.2), channel_id=1, source_target_pairs={{0,2},{1,3},{2,0},{3,1},{4,6},{5,7},{6,4},{7,5},{8,10},{9,11},{10,... | collective-permute-start | bytes 208904 | tf_op jit(solution)/shard_map/ppermute | solution.py:253
  25.0 0.0 collective-permute-done.6
  25.0 3.4 %collective-permute-done.5 = f32[136,128]{1,0:T(8,128)S(1)} collective-permute-done((f32[136,128]{1,0:T(8,128)S(1)}, f32[136,128]{1,0:T(8,128)S(1)}, u32[]{:S(2)}, u32[]{:S(2)}) %collective-permute-start.5) | collective-permute-done | bytes 69664 | tf_op jit(solution)/shard_map/ppermute | solution.py:253
  28.4 0.0 collective-permute-done.4
  28.4 3.8 %collective-permute-start.9 = (f32[136,128]{1,0:T(8,128)S(1)}, f32[136,128]{1,0:T(8,128)S(1)}, u32[]{:S(2)}, u32[]{:S(2)}) collective-permute-start(f32[136,128]{1,0:T(8,128)S(1)} %add_add_fusion.1), channel_id=1, source_target_pairs={{0,12},{1,13},{2,14},{3,15},{4,0},{5,1},{6,2},{7,3},{8,4},{9,5},{1... | collective-permute-start | bytes 208904 | tf_op jit(solution)/shard_map/ppermute | solution.py:253
  32.3 0.0 collective-permute-start.8
  32.3 1.3 %collective-permute-start.7 = (f32[136,128]{1,0:T(8,128)S(1)}, f32[136,128]{1,0:T(8,128)S(1)}, u32[]{:S(2)}, u32[]{:S(2)}) collective-permute-start(f32[136,128]{1,0:T(8,128)S(1)} %add_add_fusion.1), channel_id=1, source_target_pairs={{0,8},{1,9},{2,10},{3,11},{4,12},{5,13},{6,14},{7,15},{8,0},{9,1},... | collective-permute-start | bytes 208904 | tf_op jit(solution)/shard_map/ppermute | solution.py:253
  33.6 0.1 collective-permute-done.9
  33.6 3.7 %collective-permute-done.8 = f32[136,128]{1,0:T(8,128)S(1)} collective-permute-done((f32[136,128]{1,0:T(8,128)S(1)}, f32[136,128]{1,0:T(8,128)S(1)}, u32[]{:S(2)}, u32[]{:S(2)}) %collective-permute-start.8) | collective-permute-done | bytes 69664 | tf_op jit(solution)/shard_map/ppermute | solution.py:253
  37.4 0.0 collective-permute-done.7
  37.4 4.8 %collective-permute-start.10 = (f32[136,128]{1,0:T(8,128)S(1)}, f32[136,128]{1,0:T(8,128)S(1)}, u32[]{:S(2)}, u32[]{:S(2)}) collective-permute-start(f32[136,128]{1,0:T(8,128)S(1)} %add_add_fusion.mine_ref), channel_id=1, source_target_pairs={{0,16},{16,0},{32,48},{48,32},{64,80},{80,64},{96,112},{112,96},{1... | collective-permute-start | bytes 208904 | tf_op jit(solution)/shard_map/ppermute | solution.py:253
  42.2 0.9 collective-permute-done.10.other_ref
  43.1 0.0 copy-done
  43.1 44.2 %core.1 = (bf16[256,256]{1,0:T(8,128)(2,1)S(1)}, f32[1,128]{1,0:T(1,128)}) custom-call(s32[1]{0:T(128)} %bitcast.parity_ref, f32[136,128]{1,0:T(8,128)S(1)} %add_add_fusion.mine_ref, f32[136,128]{1,0:T(8,128)S(1)} %collective-permute-done.10.other_ref, f32[1,128]{1,0:T(1,128)S(1)} %bitcast.4), custom_call_target="tpu_custom_call" | custom-call | tf_op jit(solution)/shard_map/core/pallas_call | solution.py:299
  87.3 5.4 %apply.1 = f32[128,16384]{1,0:T(8,128)} custom-call(s32[2]{0:T(128)S(1)} %pad_add_fusion.info_ref, bf16[256,256]{1,0:T(8,128)(2,1)S(1)} %get-tuple-element.10.coeff_ref, f32[128,16384]{1,0:T(8,128)S(1)} %get-tuple-element.11.basis_ref, f32[128,16384]{1,0:T(8,128)S(1)} %get-tuple-element.12.snap_ref), custom_call_target="tpu_custom_call" | custom-call | tf_op jit(solution)/shard_map/apply/pallas_call | solution.py:315
  (4 shorter events, 0.1 us)
Async XLA Ops:
  1.4 41.7 %copy-start = (f32[128]{0:T(128)S(1)}, f32[128]{0:T(128)}, u32[]{:S(2)}) copy-start(f32[128]{0:T(128)} %param.5) | copy-start | bytes 1540
  9.8 2.4 %collective-permute-start = (f32[136,128]{1,0:T(8,128)S(1)}, f32[136,128]{1,0:T(8,128)S(1)}, u32[]{:S(2)}, u32[]{:S(2)}) collective-permute-start(f32[136,128]{1,0:T(8,128)S(1)} %get-tuple-element.9), channel_id=1, source_target_pairs={{0,16},{16,0},{32,48},{48,32},{64,80},{80,64},{96,112},{112,96},{1... | collective-permute-start | bytes 208904 | tf_op jit(solution)/shard_map/ppermute | solution.py:253
  12.2 4.6 %collective-permute-start.3 = (f32[136,128]{1,0:T(8,128)S(1)}, f32[136,128]{1,0:T(8,128)S(1)}, u32[]{:S(2)}, u32[]{:S(2)}) collective-permute-start(f32[136,128]{1,0:T(8,128)S(1)} %add.35), channel_id=1, source_target_pairs={{0,96},{16,112},{32,0},{48,16},{64,32},{80,48},{96,64},{112,80},{1... | collective-permute-start | bytes 208904 | tf_op jit(solution)/shard_map/ppermute | solution.py:253
  15.1 5.2 %collective-permute-start.2 = (f32[136,128]{1,0:T(8,128)S(1)}, f32[136,128]{1,0:T(8,128)S(1)}, u32[]{:S(2)}, u32[]{:S(2)}) collective-permute-start(f32[136,128]{1,0:T(8,128)S(1)} %add.35), channel_id=1, source_target_pairs={{0,32},{16,48},{32,64},{48,80},{64,96},{80,112},{96,0},{112,16},{1... | collective-permute-start | bytes 208904 | tf_op jit(solution)/shard_map/ppermute | solution.py:253
  15.1 5.6 %collective-permute-start.1 = (f32[136,128]{1,0:T(8,128)S(1)}, f32[136,128]{1,0:T(8,128)S(1)}, u32[]{:S(2)}, u32[]{:S(2)}) collective-permute-start(f32[136,128]{1,0:T(8,128)S(1)} %add.35), channel_id=1, source_target_pairs={{0,64},{16,80},{32,96},{48,112},{64,0},{80,16},{96,32},{112,48},{1... | collective-permute-start | bytes 208904 | tf_op jit(solution)/shard_map/ppermute | solution.py:253
  20.7 4.3 %collective-permute-start.6 = (f32[136,128]{1,0:T(8,128)S(1)}, f32[136,128]{1,0:T(8,128)S(1)}, u32[]{:S(2)}, u32[]{:S(2)}) collective-permute-start(f32[136,128]{1,0:T(8,128)S(1)} %add_add_fusion.2), channel_id=1, source_target_pairs={{0,3},{1,0},{2,1},{3,2},{4,7},{5,4},{6,5},{7,6},{8,11},{9,8},{10,9... | collective-permute-start | bytes 208904 | tf_op jit(solution)/shard_map/ppermute | solution.py:253
  23.3 5.1 %collective-permute-start.5 = (f32[136,128]{1,0:T(8,128)S(1)}, f32[136,128]{1,0:T(8,128)S(1)}, u32[]{:S(2)}, u32[]{:S(2)}) collective-permute-start(f32[136,128]{1,0:T(8,128)S(1)} %add_add_fusion.2), channel_id=1, source_target_pairs={{0,1},{1,2},{2,3},{3,0},{4,5},{5,6},{6,7},{7,4},{8,9},{9,10},{10,1... | collective-permute-start | bytes 208904 | tf_op jit(solution)/shard_map/ppermute | solution.py:253
  23.3 5.1 %collective-permute-start.4 = (f32[136,128]{1,0:T(8,128)S(1)}, f32[136,128]{1,0:T(8,128)S(1)}, u32[]{:S(2)}, u32[]{:S(2)}) collective-permute-start(f32[136,128]{1,0:T(8,128)S(1)} %add_add_fusion.2), channel_id=1, source_target_pairs={{0,2},{1,3},{2,0},{3,1},{4,6},{5,7},{6,4},{7,5},{8,10},{9,11},{10,... | collective-permute-start | bytes 208904 | tf_op jit(solution)/shard_map/ppermute | solution.py:253
  28.4 5.2 %collective-permute-start.9 = (f32[136,128]{1,0:T(8,128)S(1)}, f32[136,128]{1,0:T(8,128)S(1)}, u32[]{:S(2)}, u32[]{:S(2)}) collective-permute-start(f32[136,128]{1,0:T(8,128)S(1)} %add_add_fusion.1), channel_id=1, source_target_pairs={{0,12},{1,13},{2,14},{3,15},{4,0},{5,1},{6,2},{7,3},{8,4},{9,5},{1... | collective-permute-start | bytes 208904 | tf_op jit(solution)/shard_map/ppermute | solution.py:253
  32.3 5.1 %collective-permute-start.8 = (f32[136,128]{1,0:T(8,128)S(1)}, f32[136,128]{1,0:T(8,128)S(1)}, u32[]{:S(2)}, u32[]{:S(2)}) collective-permute-start(f32[136,128]{1,0:T(8,128)S(1)} %add_add_fusion.1), channel_id=1, source_target_pairs={{0,4},{1,5},{2,6},{3,7},{4,8},{5,9},{6,10},{7,11},{8,12},{9,13},{1... | collective-permute-start | bytes 208904 | tf_op jit(solution)/shard_map/ppermute | solution.py:253
  32.3 5.1 %collective-permute-start.7 = (f32[136,128]{1,0:T(8,128)S(1)}, f32[136,128]{1,0:T(8,128)S(1)}, u32[]{:S(2)}, u32[]{:S(2)}) collective-permute-start(f32[136,128]{1,0:T(8,128)S(1)} %add_add_fusion.1), channel_id=1, source_target_pairs={{0,8},{1,9},{2,10},{3,11},{4,12},{5,13},{6,14},{7,15},{8,0},{9,1},... | collective-permute-start | bytes 208904 | tf_op jit(solution)/shard_map/ppermute | solution.py:253
  37.4 5.7 %collective-permute-start.10 = (f32[136,128]{1,0:T(8,128)S(1)}, f32[136,128]{1,0:T(8,128)S(1)}, u32[]{:S(2)}, u32[]{:S(2)}) collective-permute-start(f32[136,128]{1,0:T(8,128)S(1)} %add_add_fusion.mine_ref), channel_id=1, source_target_pairs={{0,16},{16,0},{32,48},{48,32},{64,80},{80,64},{96,112},{112,96},{1... | collective-permute-start | bytes 208904 | tf_op jit(solution)/shard_map/ppermute | solution.py:253

commit v3 on v2

--- a/solution.py
+++ b/solution.py
@@ -45,7 +45,7 @@
 
 
 def gram_kernel(
-    info_ref, basis_hbm, snap_hbm, mine_ref, other_ref, basis_buf, snap_buf, arrived, even_acc, cross_acc, energy
+    wet_ref, basis_hbm, snap_hbm, mine_ref, other_ref, basis_buf, snap_buf, arrived, even_acc, cross_acc, energy
 ):
     width = basis_hbm.shape[1] // GRAM_PARTS
     copies = []
@@ -65,7 +65,7 @@
         for copy in copies[part]:
             copy.wait()
         span = pl.ds(part * width, width)
-        lead, rest = split_rows(basis_buf[:, span], snap_buf[:, span], part * width, info_ref[0])
+        lead, rest = split_rows(basis_buf[:, span], snap_buf[:, span], part * width, wet_ref[0])
         step, mixed_step = dot_nt(lead, lead), dot_nt(rest, lead)
         square = rest.astype(F32)
         square = square * square
@@ -88,11 +88,11 @@
     extra = jnp.where(
         lax.broadcasted_iota(jnp.int32, (8, MODES), 0) == 0,
         jnp.broadcast_to(diagonal, (8, MODES)),
-        jnp.full((8, MODES), info_ref[0].astype(F32)),
+        jnp.full((8, MODES), wet_ref[0].astype(F32)),
     )
     symmetric = jnp.concatenate([jnp.where(lane <= row, basis_gram, snap_gram), extra], 0)
     mixed = jnp.concatenate([gram[:MODES, MODES:], jnp.zeros((8, MODES), F32)], 0)
-    first = info_ref[1] == 0
+    first = lax.axis_index("grp") % 2 == 0
     mine_ref[...] = jnp.where(first, symmetric, mixed)
     other_ref[...] = jnp.where(first, mixed, symmetric)
 
@@ -114,7 +114,7 @@
     return terms[0]
 
 
-def inverse_factor(tiles, base):
+def factor_steps(tiles, base):
     sub = lax.broadcasted_iota(jnp.int32, (8, MODES), 0)
     lane = lax.broadcasted_iota(jnp.int32, (8, MODES), 1)
     tiles = list(tiles)
@@ -142,6 +142,7 @@
         tile = jnp.where(inside, jnp.where(lane - start == sub, 1.0, 0.0), tile)
         done = tree_sum([cols[c] * row_of(tile, c) for c in range(8)])
         finished.append(jnp.where(lane < start + 8, done, 0.0))
+        yield
         if block + 1 == len(tiles):
             break
         done_rows = [row_of(done, r) for r in range(8)]
@@ -156,8 +157,25 @@
     return finished
 
 
-def core_kernel(batches, parity_ref, mine_ref, other_ref, values_ref, coeff_ref, out_ref, frame, grown_buf):
-    first = parity_ref[0] == 0
+def run_together(*steppers):
+    results = [None] * len(steppers)
+    open_ones = dict(enumerate(steppers))
+    while open_ones:
+        for which, stepper in list(open_ones.items()):
+            try:
+                next(stepper)
+            except StopIteration as end:
+                results[which] = end.value
+                del open_ones[which]
+    return results
+
+
+def tiles_of(matrix, start, count):
+    return [matrix[start + 8 * i : start + 8 * i + 8] for i in range(count)]
+
+
+def core_kernel(batches, mine_ref, other_ref, values_ref, coeff_ref, out_ref, frame):
+    first = lax.axis_index("grp") % 2 == 0
     mine, other = mine_ref[...], other_ref[...]
     symmetric = jnp.where(first, mine, other)
     mixed = jnp.where(first, other, mine)[:MODES]
@@ -196,8 +214,13 @@
         )
         gram = dot_nt(dot_nn(remainder, gram_all, HIGHEST), remainder, HIGHEST)
         low = batch * width
-        tiles = inverse_factor(
-            [gram[low + 8 * i : low + 8 * i + 8] for i in range(width // 8)], low
+        head = jnp.where(row == lane, squares, 0.0) + dot_nn(project, project_t, HIGHEST)
+        square = dot_nt(head, head, HIGHEST) + dot_nt(
+            dot_nn(project, gram, HIGHEST), project, HIGHEST
+        )
+        tiles, inverse = run_together(
+            factor_steps(tiles_of(gram, low, width // 8), low),
+            factor_steps(tiles_of(square, 0, MODES // 8), 0),
         )
         blank = jnp.zeros((width, MODES), F32)
         factor_inv = jnp.concatenate(
@@ -205,21 +228,23 @@
         )
         factor_t = dot_nn(factor_inv, gram, HIGHEST)
         factor_t = jnp.where((row <= lane) & chosen, factor_t, 0.0)
+        factor = factor_t.T
         fresh = dot_nn(factor_inv, remainder, HIGHEST)
         right = jnp.concatenate([project, factor_t], 0)
-        right_t = jnp.concatenate([project_t, factor_t.T], 1)
+        right_t = jnp.concatenate([project_t, factor], 1)
         square_row = jnp.concatenate([squares, jnp.zeros((1, MODES), F32)], 1)
-        frame[...] = jnp.concatenate([identity, jnp.zeros((MODES, MODES), F32)], 1)
+        grown = jnp.concatenate([head, dot_nn(project, factor, HIGHEST)], 1)
+        frame[...] = dot_nn(jnp.concatenate(inverse, 0), grown, HIGHEST)
 
         def sweep(repeat, carry):
             now = frame[...]
             grown = now * square_row + dot_nn(dot_nn(now, right, HIGHEST), right_t, HIGHEST)
             square = dot_nt(grown, grown, HIGHEST)
-            inverse = inverse_factor([square[8 * i : 8 * i + 8] for i in range(MODES // 8)], 0)
+            (inverse,) = run_together(factor_steps(tiles_of(square, 0, MODES // 8), 0))
             frame[...] = dot_nn(jnp.concatenate(inverse, 0), grown, HIGHEST)
             return carry
 
-        lax.fori_loop(0, SWEEPS, sweep, 0)
+        lax.fori_loop(1, SWEEPS, sweep, 0)
         now = frame[...]
         side = dot_nn(now, right, HIGHEST)
         head = now[:, :MODES]
@@ -232,12 +257,12 @@
     out_ref[...] = jnp.sqrt(squares)
 
 
-def apply_kernel(info_ref, coeff_ref, basis_ref, snap_ref, out_hbm, buffer, sent):
+def apply_kernel(wet_ref, coeff_ref, basis_ref, snap_ref, out_hbm, buffer, sent):
     width = out_hbm.shape[1] // APPLY_PARTS
     copies = []
     for part in range(APPLY_PARTS):
         span = pl.ds(part * width, width)
-        lead, rest = split_rows(basis_ref[:, span], snap_ref[:, span], part * width, info_ref[0])
+        lead, rest = split_rows(basis_ref[:, span], snap_ref[:, span], part * width, wet_ref[0])
         both = dot_nn(coeff_ref[...], lead)
         buffer[:, span] = (both[:MODES] + both[MODES:]) + dot_nn(coeff_ref[:MODES, :], rest)
         copies.append(
@@ -275,7 +300,7 @@
 ANYWHERE = pl.BlockSpec(memory_space=pl.ANY)
 
 
-def gram_call(info, basis, snaps):
+def gram_call(wet, basis, snaps):
     cells = basis.shape[1]
     half = jax.ShapeDtypeStruct((MODES + 8, MODES), F32)
     near = jax.ShapeDtypeStruct((MODES, cells), F32)
@@ -292,25 +317,25 @@
         ],
         compiler_params=pltpu.CompilerParams(vmem_limit_bytes=GRAM_VMEM),
         name="gram",
-    )(info, basis, snaps)
-
-
-def core_call(parity, mine, other, values, batches=2):
+    )(wet, basis, snaps)
+
+
+def core_call(mine, other, values, batches=2):
     return pl.pallas_call(
         functools.partial(core_kernel, batches),
-        in_specs=[SMEM, VMEM, VMEM, VMEM],
+        in_specs=[VMEM, VMEM, VMEM],
         out_specs=[VMEM, VMEM],
         out_shape=[
             jax.ShapeDtypeStruct((2 * MODES, 2 * MODES), BF16),
             jax.ShapeDtypeStruct((1, MODES), F32),
         ],
-        scratch_shapes=[pltpu.VMEM((MODES, 2 * MODES), F32)] * 2,
+        scratch_shapes=[pltpu.VMEM((MODES, 2 * MODES), F32)],
         compiler_params=pltpu.CompilerParams(vmem_limit_bytes=CORE_VMEM),
         name="core",
-    )(parity, mine, other, values)
-
-
-def apply_call(info, coeff, basis, snaps):
+    )(mine, other, values)
+
+
+def apply_call(wet, coeff, basis, snaps):
     cells = basis.shape[1]
     return pl.pallas_call(
         apply_kernel,
@@ -323,20 +348,18 @@
         ],
         compiler_params=pltpu.CompilerParams(vmem_limit_bytes=APPLY_VMEM),
         name="apply",
-    )(info, coeff, basis, snaps)
+    )(wet, coeff, basis, snaps)
 
 
 def per_device(basis_old, values_old, snapshots, wet_counts):
     batches, batch_width, cells = snapshots.shape
     snaps = snapshots.reshape(batches * batch_width, cells)
-    parity = (lax.axis_index("grp") % 2).astype(jnp.int32)
-    info = jnp.stack([wet_counts[0], parity])
     far = pltpu.with_memory_space_constraint(basis_old, pltpu.HBM)
     far_snaps = pltpu.with_memory_space_constraint(snaps, pltpu.HBM)
-    mine, other, near_basis, near_snaps = gram_call(info, far, far_snaps)
+    mine, other, near_basis, near_snaps = gram_call(wet_counts, far, far_snaps)
     mine, other = total_over_devices(mine, other)
-    coeff, values = core_call(parity[None], mine, other, values_old[None, :], batches)
-    basis = apply_call(info, coeff, near_basis, near_snaps)
+    coeff, values = core_call(mine, other, values_old[None, :], batches)
+    basis = apply_call(wet_counts, coeff, near_basis, near_snaps)
     return basis, values[0]
 
 

time: 93 us -> 86.5 us (0.930)
  Pallas kernels: 58 us -> 51.6 us
    pallas_call x1, Pallas kernels: 44.2 us -> 39.3 us  [core_call(): pl.pallas_call(functools.partial(core_kernel, batches), in_specs=[VMEM, V...]
where the time goes in v3:
time: 86.5 us; the launch traced here: 86.4 us
  Pallas kernels  51.6 us (60%)
  starting transfers between devices  20.2 us (23%)
  waiting for transfers between devices  13 us (15%)
  between operations  1.5 us (2%)
    pallas_call x1, Pallas kernels, core_call(): pl.pallas_call(functools.partial(core_kernel, batches), in_specs=[VMEM, V...  39.3 us
    ppermute x11, starting transfers between devices, exchange(): return lax.ppermute(array, axis, [(i, move(i)) for i in range(size)])  20.2 us
    ppermute x11, waiting for transfers between devices, exchange(): return lax.ppermute(array, axis, [(i, move(i)) for i in range(size)])  13 us
    pallas_call x1, Pallas kernels, gram_call(): pl.pallas_call(gram_kernel, in_specs=[SMEM, ANYWHERE, ANYWHERE], out_spec...  7.73 us
    pallas_call x1, Pallas kernels, apply_call(): pl.pallas_call(apply_kernel, in_specs=[SMEM, VMEM, VMEM, VMEM], out_specs...  4.56 us
  transfers between devices with their start and end apart: 11, of which 7 were waited for; matrix products, arithmetic and copies ran while one was open for 0% of the time, Pallas kernels for 0%

profile of v3, /device:TPU:1, one launch (start us, length us, event | category | flops | bytes accessed | tf_op | source)
XLA Modules:
  0.0 86.4 jit_solution(1814980245193379396)
XLA Ops:
  1.3 0.0 copy-start
  1.3 7.7 %gram.1 = (f32[136,128]{1,0:T(8,128)S(1)}, f32[136,128]{1,0:T(8,128)S(1)}, f32[128,16384]{1,0:T(8,128)S(1)}, f32[128,16384]{1,0:T(8,128)S(1)}) custom-call(s32[1]{0:T(128)S(6)} %copy.6.wet_ref, f32[128,16384]{1,0:T(8,128)} %basis_hbm.1, f32[128,16384]{1,0:T(8,128)} %bitcast.4), custom_call_target="tpu_custom_call" | custom-call | tf_op jit(solution)/shard_map/gram/pallas_call | solution.py:307
  9.0 1.5 %collective-permute-start = (f32[136,128]{1,0:T(8,128)S(1)}, f32[136,128]{1,0:T(8,128)S(1)}, u32[]{:S(2)}, u32[]{:S(2)}) collective-permute-start(f32[136,128]{1,0:T(8,128)S(1)} %get-tuple-element.9), channel_id=1, source_target_pairs={{0,16},{16,0},{32,48},{48,32},{64,80},{80,64},{96,112},{112,96},{1... | collective-permute-start | bytes 208904 | tf_op jit(solution)/shard_map/ppermute | solution.py:278
  10.5 0.9 %collective-permute-done = f32[136,128]{1,0:T(8,128)S(1)} collective-permute-done((f32[136,128]{1,0:T(8,128)S(1)}, f32[136,128]{1,0:T(8,128)S(1)}, u32[]{:S(2)}, u32[]{:S(2)}) %collective-permute-start) | collective-permute-done | bytes 69664 | tf_op jit(solution)/shard_map/ppermute | solution.py:278
  11.4 2.9 %collective-permute-start.3 = (f32[136,128]{1,0:T(8,128)S(1)}, f32[136,128]{1,0:T(8,128)S(1)}, u32[]{:S(2)}, u32[]{:S(2)}) collective-permute-start(f32[136,128]{1,0:T(8,128)S(1)} %add.30), channel_id=1, source_target_pairs={{0,96},{16,112},{32,0},{48,16},{64,32},{80,48},{96,64},{112,80},{1... | collective-permute-start | bytes 208904 | tf_op jit(solution)/shard_map/ppermute | solution.py:278
  14.3 0.0 collective-permute-start.2
  14.3 1.6 %collective-permute-start.1 = (f32[136,128]{1,0:T(8,128)S(1)}, f32[136,128]{1,0:T(8,128)S(1)}, u32[]{:S(2)}, u32[]{:S(2)}) collective-permute-start(f32[136,128]{1,0:T(8,128)S(1)} %add.30), channel_id=1, source_target_pairs={{0,64},{16,80},{32,96},{48,112},{64,0},{80,16},{96,32},{112,48},{1... | collective-permute-start | bytes 208904 | tf_op jit(solution)/shard_map/ppermute | solution.py:278
  16.0 0.0 collective-permute-done.3
  16.0 3.6 %collective-permute-done.2 = f32[136,128]{1,0:T(8,128)S(1)} collective-permute-done((f32[136,128]{1,0:T(8,128)S(1)}, f32[136,128]{1,0:T(8,128)S(1)}, u32[]{:S(2)}, u32[]{:S(2)}) %collective-permute-start.2) | collective-permute-done | bytes 69664 | tf_op jit(solution)/shard_map/ppermute | solution.py:278
  19.5 0.4 collective-permute-done.1
  20.0 2.6 %collective-permute-start.6 = (f32[136,128]{1,0:T(8,128)S(1)}, f32[136,128]{1,0:T(8,128)S(1)}, u32[]{:S(2)}, u32[]{:S(2)}) collective-permute-start(f32[136,128]{1,0:T(8,128)S(1)} %add_add_fusion.2), channel_id=1, source_target_pairs={{0,3},{1,0},{2,1},{3,2},{4,7},{5,4},{6,5},{7,6},{8,11},{9,8},{10,9... | collective-permute-start | bytes 208904 | tf_op jit(solution)/shard_map/ppermute | solution.py:278
  22.5 0.0 collective-permute-start.5
  22.5 1.7 %collective-permute-start.4 = (f32[136,128]{1,0:T(8,128)S(1)}, f32[136,128]{1,0:T(8,128)S(1)}, u32[]{:S(2)}, u32[]{:S(2)}) collective-permute-start(f32[136,128]{1,0:T(8,128)S(1)} %add_add_fusion.2), channel_id=1, source_target_pairs={{0,2},{1,3},{2,0},{3,1},{4,6},{5,7},{6,4},{7,5},{8,10},{9,11},{10,... | collective-permute-start | bytes 208904 | tf_op jit(solution)/shard_map/ppermute | solution.py:278
  24.3 0.0 collective-permute-done.6
  24.3 3.4 %collective-permute-done.5 = f32[136,128]{1,0:T(8,128)S(1)} collective-permute-done((f32[136,128]{1,0:T(8,128)S(1)}, f32[136,128]{1,0:T(8,128)S(1)}, u32[]{:S(2)}, u32[]{:S(2)}) %collective-permute-start.5) | collective-permute-done | bytes 69664 | tf_op jit(solution)/shard_map/ppermute | solution.py:278
  27.7 0.0 collective-permute-done.4
  27.7 3.8 %collective-permute-start.9 = (f32[136,128]{1,0:T(8,128)S(1)}, f32[136,128]{1,0:T(8,128)S(1)}, u32[]{:S(2)}, u32[]{:S(2)}) collective-permute-start(f32[136,128]{1,0:T(8,128)S(1)} %add_add_fusion.1), channel_id=1, source_target_pairs={{0,12},{1,13},{2,14},{3,15},{4,0},{5,1},{6,2},{7,3},{8,4},{9,5},{1... | collective-permute-start | bytes 208904 | tf_op jit(solution)/shard_map/ppermute | solution.py:278
  31.5 0.0 collective-permute-start.8
  31.5 1.3 %collective-permute-start.7 = (f32[136,128]{1,0:T(8,128)S(1)}, f32[136,128]{1,0:T(8,128)S(1)}, u32[]{:S(2)}, u32[]{:S(2)}) collective-permute-start(f32[136,128]{1,0:T(8,128)S(1)} %add_add_fusion.1), channel_id=1, source_target_pairs={{0,8},{1,9},{2,10},{3,11},{4,12},{5,13},{6,14},{7,15},{8,0},{9,1},... | collective-permute-start | bytes 208904 | tf_op jit(solution)/shard_map/ppermute | solution.py:278
  32.8 0.1 collective-permute-done.9
  32.9 3.7 %collective-permute-done.8 = f32[136,128]{1,0:T(8,128)S(1)} collective-permute-done((f32[136,128]{1,0:T(8,128)S(1)}, f32[136,128]{1,0:T(8,128)S(1)}, u32[]{:S(2)}, u32[]{:S(2)}) %collective-permute-start.8) | collective-permute-done | bytes 69664 | tf_op jit(solution)/shard_map/ppermute | solution.py:278
  36.6 0.0 collective-permute-done.7
  36.6 4.8 %collective-permute-start.10 = (f32[136,128]{1,0:T(8,128)S(1)}, f32[136,128]{1,0:T(8,128)S(1)}, u32[]{:S(2)}, u32[]{:S(2)}) collective-permute-start(f32[136,128]{1,0:T(8,128)S(1)} %add_add_fusion.mine_ref), channel_id=1, source_target_pairs={{0,16},{16,0},{32,48},{48,32},{64,80},{80,64},{96,112},{112,96},{1... | collective-permute-start | bytes 208904 | tf_op jit(solution)/shard_map/ppermute | solution.py:278
  41.4 0.9 %collective-permute-done.10.other_ref = f32[136,128]{1,0:T(8,128)S(1)} collective-permute-done((f32[136,128]{1,0:T(8,128)S(1)}, f32[136,128]{1,0:T(8,128)S(1)}, u32[]{:S(2)}, u32[]{:S(2)}) %collective-permute-start.10) | collective-permute-done | bytes 69664 | tf_op jit(solution)/shard_map/ppermute | solution.py:278
  42.3 0.0 copy-done
  42.3 39.3 %core.1 = (bf16[256,256]{1,0:T(8,128)(2,1)S(1)}, f32[1,128]{1,0:T(1,128)}) custom-call(f32[136,128]{1,0:T(8,128)S(1)} %add_add_fusion.mine_ref, f32[136,128]{1,0:T(8,128)S(1)} %collective-permute-done.10.other_ref, f32[1,128]{1,0:T(1,128)S(1)} %bitcast.3), custom_call_target="tpu_custom_call" | custom-call | tf_op jit(solution)/shard_map/core/pallas_call | solution.py:324
  81.7 4.6 %apply.1 = f32[128,16384]{1,0:T(8,128)} custom-call(s32[1]{0:T(128)S(6)} %copy.6.wet_ref, bf16[256,256]{1,0:T(8,128)(2,1)S(1)} %get-tuple-element.10.coeff_ref, f32[128,16384]{1,0:T(8,128)S(1)} %get-tuple-element.11.basis_ref, f32[128,16384]{1,0:T(8,128)S(1)} %get-tuple-element.12.snap_ref), custom_call_target="tpu_custom_call" | custom-call | tf_op jit(solution)/shard_map/apply/pallas_call | solution.py:340
  (4 shorter events, 0.1 us)
Async XLA Ops:
  1.3 41.1 %copy-start = (f32[128]{0:T(128)S(1)}, f32[128]{0:T(128)}, u32[]{:S(2)}) copy-start(f32[128]{0:T(128)} %param.5) | copy-start | bytes 1540
  9.0 2.4 %collective-permute-start = (f32[136,128]{1,0:T(8,128)S(1)}, f32[136,128]{1,0:T(8,128)S(1)}, u32[]{:S(2)}, u32[]{:S(2)}) collective-permute-start(f32[136,128]{1,0:T(8,128)S(1)} %get-tuple-element.9), channel_id=1, source_target_pairs={{0,16},{16,0},{32,48},{48,32},{64,80},{80,64},{96,112},{112,96},{1... | collective-permute-start | bytes 208904 | tf_op jit(solution)/shard_map/ppermute | solution.py:278
  11.4 4.6 %collective-permute-start.3 = (f32[136,128]{1,0:T(8,128)S(1)}, f32[136,128]{1,0:T(8,128)S(1)}, u32[]{:S(2)}, u32[]{:S(2)}) collective-permute-start(f32[136,128]{1,0:T(8,128)S(1)} %add.30), channel_id=1, source_target_pairs={{0,96},{16,112},{32,0},{48,16},{64,32},{80,48},{96,64},{112,80},{1... | collective-permute-start | bytes 208904 | tf_op jit(solution)/shard_map/ppermute | solution.py:278
  14.3 5.2 %collective-permute-start.2 = (f32[136,128]{1,0:T(8,128)S(1)}, f32[136,128]{1,0:T(8,128)S(1)}, u32[]{:S(2)}, u32[]{:S(2)}) collective-permute-start(f32[136,128]{1,0:T(8,128)S(1)} %add.30), channel_id=1, source_target_pairs={{0,32},{16,48},{32,64},{48,80},{64,96},{80,112},{96,0},{112,16},{1... | collective-permute-start | bytes 208904 | tf_op jit(solution)/shard_map/ppermute | solution.py:278
  14.3 5.6 %collective-permute-start.1 = (f32[136,128]{1,0:T(8,128)S(1)}, f32[136,128]{1,0:T(8,128)S(1)}, u32[]{:S(2)}, u32[]{:S(2)}) collective-permute-start(f32[136,128]{1,0:T(8,128)S(1)} %add.30), channel_id=1, source_target_pairs={{0,64},{16,80},{32,96},{48,112},{64,0},{80,16},{96,32},{112,48},{1... | collective-permute-start | bytes 208904 | tf_op jit(solution)/shard_map/ppermute | solution.py:278
  20.0 4.3 %collective-permute-start.6 = (f32[136,128]{1,0:T(8,128)S(1)}, f32[136,128]{1,0:T(8,128)S(1)}, u32[]{:S(2)}, u32[]{:S(2)}) collective-permute-start(f32[136,128]{1,0:T(8,128)S(1)} %add_add_fusion.2), channel_id=1, source_target_pairs={{0,3},{1,0},{2,1},{3,2},{4,7},{5,4},{6,5},{7,6},{8,11},{9,8},{10,9... | collective-permute-start | bytes 208904 | tf_op jit(solution)/shard_map/ppermute | solution.py:278
  22.5 5.1 %collective-permute-start.5 = (f32[136,128]{1,0:T(8,128)S(1)}, f32[136,128]{1,0:T(8,128)S(1)}, u32[]{:S(2)}, u32[]{:S(2)}) collective-permute-start(f32[136,128]{1,0:T(8,128)S(1)} %add_add_fusion.2), channel_id=1, source_target_pairs={{0,1},{1,2},{2,3},{3,0},{4,5},{5,6},{6,7},{7,4},{8,9},{9,10},{10,1... | collective-permute-start | bytes 208904 | tf_op jit(solution)/shard_map/ppermute | solution.py:278
  22.5 5.1 %collective-permute-start.4 = (f32[136,128]{1,0:T(8,128)S(1)}, f32[136,128]{1,0:T(8,128)S(1)}, u32[]{:S(2)}, u32[]{:S(2)}) collective-permute-start(f32[136,128]{1,0:T(8,128)S(1)} %add_add_fusion.2), channel_id=1, source_target_pairs={{0,2},{1,3},{2,0},{3,1},{4,6},{5,7},{6,4},{7,5},{8,10},{9,11},{10,... | collective-permute-start | bytes 208904 | tf_op jit(solution)/shard_map/ppermute | solution.py:278
  27.7 5.2 %collective-permute-start.9 = (f32[136,128]{1,0:T(8,128)S(1)}, f32[136,128]{1,0:T(8,128)S(1)}, u32[]{:S(2)}, u32[]{:S(2)}) collective-permute-start(f32[136,128]{1,0:T(8,128)S(1)} %add_add_fusion.1), channel_id=1, source_target_pairs={{0,12},{1,13},{2,14},{3,15},{4,0},{5,1},{6,2},{7,3},{8,4},{9,5},{1... | collective-permute-start | bytes 208904 | tf_op jit(solution)/shard_map/ppermute | solution.py:278
  31.5 5.1 %collective-permute-start.8 = (f32[136,128]{1,0:T(8,128)S(1)}, f32[136,128]{1,0:T(8,128)S(1)}, u32[]{:S(2)}, u32[]{:S(2)}) collective-permute-start(f32[136,128]{1,0:T(8,128)S(1)} %add_add_fusion.1), channel_id=1, source_target_pairs={{0,4},{1,5},{2,6},{3,7},{4,8},{5,9},{6,10},{7,11},{8,12},{9,13},{1... | collective-permute-start | bytes 208904 | tf_op jit(solution)/shard_map/ppermute | solution.py:278
  31.5 5.1 %collective-permute-start.7 = (f32[136,128]{1,0:T(8,128)S(1)}, f32[136,128]{1,0:T(8,128)S(1)}, u32[]{:S(2)}, u32[]{:S(2)}) collective-permute-start(f32[136,128]{1,0:T(8,128)S(1)} %add_add_fusion.1), channel_id=1, source_target_pairs={{0,8},{1,9},{2,10},{3,11},{4,12},{5,13},{6,14},{7,15},{8,0},{9,1},... | collective-permute-start | bytes 208904 | tf_op jit(solution)/shard_map/ppermute | solution.py:278
  36.6 5.7 %collective-permute-start.10 = (f32[136,128]{1,0:T(8,128)S(1)}, f32[136,128]{1,0:T(8,128)S(1)}, u32[]{:S(2)}, u32[]{:S(2)}) collective-permute-start(f32[136,128]{1,0:T(8,128)S(1)} %add_add_fusion.mine_ref), channel_id=1, source_target_pairs={{0,16},{16,0},{32,48},{48,32},{64,80},{80,64},{96,112},{112,96},{1... | collective-permute-start | bytes 208904 | tf_op jit(solution)/shard_map/ppermute | solution.py:278

commit v4 on v3

--- a/solution.py
+++ b/solution.py
@@ -9,6 +9,7 @@
 
 BLOCK = 128
 SWEEPS = 3
+EARLY_TILES = 3
 MODES = 128
 GRAM_PARTS = 8
 APPLY_PARTS = 16
@@ -114,7 +115,7 @@
     return terms[0]
 
 
-def factor_steps(tiles, base):
+def factor_steps(tiles, base, never):
     sub = lax.broadcasted_iota(jnp.int32, (8, MODES), 0)
     lane = lax.broadcasted_iota(jnp.int32, (8, MODES), 1)
     tiles = list(tiles)
@@ -123,13 +124,21 @@
         start = base + 8 * block
         tile = tiles[block]
         cols = [lane_of(tile, start + j) for j in range(8)]
-        pivots = None
+        early = {}
+        for other in range(block + 1, min(len(tiles), block + 1 + EARLY_TILES)):
+            early[other] = [lane_of(tiles[other], start + c) for c in range(8)]
+            cols = [jnp.where(never, e, c) for e, c in zip(early[other], cols)]
+        pivot = row_of(cols[0], 0)
+        pivots = pivot
         for k in range(8):
-            pivot = row_of(cols[k], k)
-            pivots = pivot if pivots is None else jnp.where(sub >= k, pivot, pivots)
             unit = jnp.where(sub == k, 1.0, 0.0)
             if k < 7:
-                scale = jnp.where(sub > k, cols[k], 0.0) * (1.0 / pivot)
+                inverse = 1.0 / pivot
+                scale = jnp.where(sub > k, cols[k], 0.0) * inverse
+                pivot = row_of(cols[k + 1], k + 1) - (row_of(cols[k], k + 1) * inverse) * row_of(
+                    cols[k + 1], k
+                )
+                pivots = jnp.where(sub > k, pivot, pivots)
                 for j in range(8):
                     if j != k:
                         cols[j] = cols[j] - scale * row_of(cols[j], k)
@@ -151,9 +160,11 @@
         ]
         for other in range(block + 1, len(tiles)):
             kept = jnp.where(inside, 0.0, tiles[other])
-            tiles[other] = kept - tree_sum(
-                [lane_of(tiles[other], start + c) * update[c] for c in range(8)]
-            )
+            if other in early:
+                across = early[other]
+            else:
+                across = [lane_of(tiles[other], start + c) for c in range(8)]
+            tiles[other] = kept - tree_sum([across[c] * update[c] for c in range(8)])
     return finished
 
 
@@ -184,6 +195,7 @@
     identity = jnp.where(row == lane, 1.0, 0.0)
     wet_total = symmetric[MODES + 1 : MODES + 2, 0:1] * BLOCK
     weight = 1.0 / wet_total
+    never = jnp.broadcast_to(wet_total, (8, MODES)) < 0.0
     diagonal = symmetric[MODES : MODES + 1, :] * weight
     symmetric = symmetric[:MODES] * weight
     flipped = symmetric.T
@@ -219,8 +231,8 @@
             dot_nn(project, gram, HIGHEST), project, HIGHEST
         )
         tiles, inverse = run_together(
-            factor_steps(tiles_of(gram, low, width // 8), low),
-            factor_steps(tiles_of(square, 0, MODES // 8), 0),
+            factor_steps(tiles_of(gram, low, width // 8), low, never),
+            factor_steps(tiles_of(square, 0, MODES // 8), 0, never),
         )
         blank = jnp.zeros((width, MODES), F32)
         factor_inv = jnp.concatenate(
@@ -240,7 +252,7 @@
             now = frame[...]
             grown = now * square_row + dot_nn(dot_nn(now, right, HIGHEST), right_t, HIGHEST)
             square = dot_nt(grown, grown, HIGHEST)
-            (inverse,) = run_together(factor_steps(tiles_of(square, 0, MODES // 8), 0))
+            (inverse,) = run_together(factor_steps(tiles_of(square, 0, MODES // 8), 0, never))
             frame[...] = dot_nn(jnp.concatenate(inverse, 0), grown, HIGHEST)
             return carry
 

time: 86.5 us -> 78.5 us (0.908)
  Pallas kernels: 51.6 us -> 43.6 us
    pallas_call x1, Pallas kernels: 39.3 us -> 31.3 us  [core_call(): pl.pallas_call(functools.partial(core_kernel, batches), in_specs=[VMEM, V...]
where the time goes in v4:
time: 78.5 us; the launch traced here: 78.4 us
  Pallas kernels  43.6 us (56%)
  starting transfers between devices  20.2 us (26%)
  waiting for transfers between devices  13 us (17%)
  between operations  1.5 us (2%)
    pallas_call x1, Pallas kernels, core_call(): pl.pallas_call(functools.partial(core_kernel, batches), in_specs=[VMEM, V...  31.3 us
    ppermute x11, starting transfers between devices, exchange(): return lax.ppermute(array, axis, [(i, move(i)) for i in range(size)])  20.2 us
    ppermute x11, waiting for transfers between devices, exchange(): return lax.ppermute(array, axis, [(i, move(i)) for i in range(size)])  13 us
    pallas_call x1, Pallas kernels, gram_call(): pl.pallas_call(gram_kernel, in_specs=[SMEM, ANYWHERE, ANYWHERE], out_spec...  7.73 us
    pallas_call x1, Pallas kernels, apply_call(): pl.pallas_call(apply_kernel, in_specs=[SMEM, VMEM, VMEM, VMEM], out_specs...  4.57 us
  transfers between devices with their start and end apart: 11, of which 7 were waited for; matrix products, arithmetic and copies ran while one was open for 0% of the time, Pallas kernels for 0%

profile of v4, /device:TPU:1, one launch (start us, length us, event | category | flops | bytes accessed | tf_op | source)
XLA Modules:
  0.0 78.4 jit_solution(6827721422879914510)
XLA Ops:
  1.3 0.0 copy-start
  1.3 7.7 %gram.1 = (f32[136,128]{1,0:T(8,128)S(1)}, f32[136,128]{1,0:T(8,128)S(1)}, f32[128,16384]{1,0:T(8,128)S(1)}, f32[128,16384]{1,0:T(8,128)S(1)}) custom-call(s32[1]{0:T(128)S(6)} %copy.6.wet_ref, f32[128,16384]{1,0:T(8,128)} %basis_hbm.1, f32[128,16384]{1,0:T(8,128)} %bitcast.4), custom_call_target="tpu_custom_call" | custom-call | tf_op jit(solution)/shard_map/gram/pallas_call | solution.py:319
  9.0 1.5 %collective-permute-start = (f32[136,128]{1,0:T(8,128)S(1)}, f32[136,128]{1,0:T(8,128)S(1)}, u32[]{:S(2)}, u32[]{:S(2)}) collective-permute-start(f32[136,128]{1,0:T(8,128)S(1)} %get-tuple-element.9), channel_id=1, source_target_pairs={{0,16},{16,0},{32,48},{48,32},{64,80},{80,64},{96,112},{112,96},{1... | collective-permute-start | bytes 208904 | tf_op jit(solution)/shard_map/ppermute | solution.py:290
  10.5 0.9 %collective-permute-done = f32[136,128]{1,0:T(8,128)S(1)} collective-permute-done((f32[136,128]{1,0:T(8,128)S(1)}, f32[136,128]{1,0:T(8,128)S(1)}, u32[]{:S(2)}, u32[]{:S(2)}) %collective-permute-start) | collective-permute-done | bytes 69664 | tf_op jit(solution)/shard_map/ppermute | solution.py:290
  11.4 2.9 %collective-permute-start.3 = (f32[136,128]{1,0:T(8,128)S(1)}, f32[136,128]{1,0:T(8,128)S(1)}, u32[]{:S(2)}, u32[]{:S(2)}) collective-permute-start(f32[136,128]{1,0:T(8,128)S(1)} %add.30), channel_id=1, source_target_pairs={{0,96},{16,112},{32,0},{48,16},{64,32},{80,48},{96,64},{112,80},{1... | collective-permute-start | bytes 208904 | tf_op jit(solution)/shard_map/ppermute | solution.py:290
  14.3 0.0 collective-permute-start.2
  14.3 1.6 %collective-permute-start.1 = (f32[136,128]{1,0:T(8,128)S(1)}, f32[136,128]{1,0:T(8,128)S(1)}, u32[]{:S(2)}, u32[]{:S(2)}) collective-permute-start(f32[136,128]{1,0:T(8,128)S(1)} %add.30), channel_id=1, source_target_pairs={{0,64},{16,80},{32,96},{48,112},{64,0},{80,16},{96,32},{112,48},{1... | collective-permute-start | bytes 208904 | tf_op jit(solution)/shard_map/ppermute | solution.py:290
  16.0 0.0 collective-permute-done.3
  16.0 3.6 %collective-permute-done.2 = f32[136,128]{1,0:T(8,128)S(1)} collective-permute-done((f32[136,128]{1,0:T(8,128)S(1)}, f32[136,128]{1,0:T(8,128)S(1)}, u32[]{:S(2)}, u32[]{:S(2)}) %collective-permute-start.2) | collective-permute-done | bytes 69664 | tf_op jit(solution)/shard_map/ppermute | solution.py:290
  19.5 0.4 collective-permute-done.1
  20.0 2.6 %collective-permute-start.6 = (f32[136,128]{1,0:T(8,128)S(1)}, f32[136,128]{1,0:T(8,128)S(1)}, u32[]{:S(2)}, u32[]{:S(2)}) collective-permute-start(f32[136,128]{1,0:T(8,128)S(1)} %add_add_fusion.2), channel_id=1, source_target_pairs={{0,3},{1,0},{2,1},{3,2},{4,7},{5,4},{6,5},{7,6},{8,11},{9,8},{10,9... | collective-permute-start | bytes 208904 | tf_op jit(solution)/shard_map/ppermute | solution.py:290
  22.5 0.0 collective-permute-start.5
  22.5 1.7 %collective-permute-start.4 = (f32[136,128]{1,0:T(8,128)S(1)}, f32[136,128]{1,0:T(8,128)S(1)}, u32[]{:S(2)}, u32[]{:S(2)}) collective-permute-start(f32[136,128]{1,0:T(8,128)S(1)} %add_add_fusion.2), channel_id=1, source_target_pairs={{0,2},{1,3},{2,0},{3,1},{4,6},{5,7},{6,4},{7,5},{8,10},{9,11},{10,... | collective-permute-start | bytes 208904 | tf_op jit(solution)/shard_map/ppermute | solution.py:290
  24.3 0.0 collective-permute-done.6
  24.3 3.4 %collective-permute-done.5 = f32[136,128]{1,0:T(8,128)S(1)} collective-permute-done((f32[136,128]{1,0:T(8,128)S(1)}, f32[136,128]{1,0:T(8,128)S(1)}, u32[]{:S(2)}, u32[]{:S(2)}) %collective-permute-start.5) | collective-permute-done | bytes 69664 | tf_op jit(solution)/shard_map/ppermute | solution.py:290
  27.7 0.0 collective-permute-done.4
  27.7 3.8 %collective-permute-start.9 = (f32[136,128]{1,0:T(8,128)S(1)}, f32[136,128]{1,0:T(8,128)S(1)}, u32[]{:S(2)}, u32[]{:S(2)}) collective-permute-start(f32[136,128]{1,0:T(8,128)S(1)} %add_add_fusion.1), channel_id=1, source_target_pairs={{0,12},{1,13},{2,14},{3,15},{4,0},{5,1},{6,2},{7,3},{8,4},{9,5},{1... | collective-permute-start | bytes 208904 | tf_op jit(solution)/shard_map/ppermute | solution.py:290
  31.5 0.0 collective-permute-start.8
  31.5 1.3 %collective-permute-start.7 = (f32[136,128]{1,0:T(8,128)S(1)}, f32[136,128]{1,0:T(8,128)S(1)}, u32[]{:S(2)}, u32[]{:S(2)}) collective-permute-start(f32[136,128]{1,0:T(8,128)S(1)} %add_add_fusion.1), channel_id=1, source_target_pairs={{0,8},{1,9},{2,10},{3,11},{4,12},{5,13},{6,14},{7,15},{8,0},{9,1},... | collective-permute-start | bytes 208904 | tf_op jit(solution)/shard_map/ppermute | solution.py:290
  32.8 0.1 collective-permute-done.9
  32.9 3.7 %collective-permute-done.8 = f32[136,128]{1,0:T(8,128)S(1)} collective-permute-done((f32[136,128]{1,0:T(8,128)S(1)}, f32[136,128]{1,0:T(8,128)S(1)}, u32[]{:S(2)}, u32[]{:S(2)}) %collective-permute-start.8) | collective-permute-done | bytes 69664 | tf_op jit(solution)/shard_map/ppermute | solution.py:290
  36.6 0.0 collective-permute-done.7
  36.6 4.8 %collective-permute-start.10 = (f32[136,128]{1,0:T(8,128)S(1)}, f32[136,128]{1,0:T(8,128)S(1)}, u32[]{:S(2)}, u32[]{:S(2)}) collective-permute-start(f32[136,128]{1,0:T(8,128)S(1)} %add_add_fusion.mine_ref), channel_id=1, source_target_pairs={{0,16},{16,0},{32,48},{48,32},{64,80},{80,64},{96,112},{112,96},{1... | collective-permute-start | bytes 208904 | tf_op jit(solution)/shard_map/ppermute | solution.py:290
  41.4 0.9 %collective-permute-done.10.other_ref = f32[136,128]{1,0:T(8,128)S(1)} collective-permute-done((f32[136,128]{1,0:T(8,128)S(1)}, f32[136,128]{1,0:T(8,128)S(1)}, u32[]{:S(2)}, u32[]{:S(2)}) %collective-permute-start.10) | collective-permute-done | bytes 69664 | tf_op jit(solution)/shard_map/ppermute | solution.py:290
  42.3 0.0 copy-done
  42.3 31.3 %core.1 = (bf16[256,256]{1,0:T(8,128)(2,1)S(1)}, f32[1,128]{1,0:T(1,128)}) custom-call(f32[136,128]{1,0:T(8,128)S(1)} %add_add_fusion.mine_ref, f32[136,128]{1,0:T(8,128)S(1)} %collective-permute-done.10.other_ref, f32[1,128]{1,0:T(1,128)S(1)} %bitcast.3), custom_call_target="tpu_custom_call" | custom-call | tf_op jit(solution)/shard_map/core/pallas_call | solution.py:336
  73.6 4.6 %apply.1 = f32[128,16384]{1,0:T(8,128)} custom-call(s32[1]{0:T(128)S(6)} %copy.6.wet_ref, bf16[256,256]{1,0:T(8,128)(2,1)S(1)} %get-tuple-element.10.coeff_ref, f32[128,16384]{1,0:T(8,128)S(1)} %get-tuple-element.11.basis_ref, f32[128,16384]{1,0:T(8,128)S(1)} %get-tuple-element.12.snap_ref), custom_call_target="tpu_custom_call" | custom-call | tf_op jit(solution)/shard_map/apply/pallas_call | solution.py:352
  (4 shorter events, 0.1 us)
Async XLA Ops:
  1.3 41.1 %copy-start = (f32[128]{0:T(128)S(1)}, f32[128]{0:T(128)}, u32[]{:S(2)}) copy-start(f32[128]{0:T(128)} %param.5) | copy-start | bytes 1540
  9.0 2.4 %collective-permute-start = (f32[136,128]{1,0:T(8,128)S(1)}, f32[136,128]{1,0:T(8,128)S(1)}, u32[]{:S(2)}, u32[]{:S(2)}) collective-permute-start(f32[136,128]{1,0:T(8,128)S(1)} %get-tuple-element.9), channel_id=1, source_target_pairs={{0,16},{16,0},{32,48},{48,32},{64,80},{80,64},{96,112},{112,96},{1... | collective-permute-start | bytes 208904 | tf_op jit(solution)/shard_map/ppermute | solution.py:290
  11.4 4.6 %collective-permute-start.3 = (f32[136,128]{1,0:T(8,128)S(1)}, f32[136,128]{1,0:T(8,128)S(1)}, u32[]{:S(2)}, u32[]{:S(2)}) collective-permute-start(f32[136,128]{1,0:T(8,128)S(1)} %add.30), channel_id=1, source_target_pairs={{0,96},{16,112},{32,0},{48,16},{64,32},{80,48},{96,64},{112,80},{1... | collective-permute-start | bytes 208904 | tf_op jit(solution)/shard_map/ppermute | solution.py:290
  14.3 5.2 %collective-permute-start.2 = (f32[136,128]{1,0:T(8,128)S(1)}, f32[136,128]{1,0:T(8,128)S(1)}, u32[]{:S(2)}, u32[]{:S(2)}) collective-permute-start(f32[136,128]{1,0:T(8,128)S(1)} %add.30), channel_id=1, source_target_pairs={{0,32},{16,48},{32,64},{48,80},{64,96},{80,112},{96,0},{112,16},{1... | collective-permute-start | bytes 208904 | tf_op jit(solution)/shard_map/ppermute | solution.py:290
  14.3 5.6 %collective-permute-start.1 = (f32[136,128]{1,0:T(8,128)S(1)}, f32[136,128]{1,0:T(8,128)S(1)}, u32[]{:S(2)}, u32[]{:S(2)}) collective-permute-start(f32[136,128]{1,0:T(8,128)S(1)} %add.30), channel_id=1, source_target_pairs={{0,64},{16,80},{32,96},{48,112},{64,0},{80,16},{96,32},{112,48},{1... | collective-permute-start | bytes 208904 | tf_op jit(solution)/shard_map/ppermute | solution.py:290
  20.0 4.3 %collective-permute-start.6 = (f32[136,128]{1,0:T(8,128)S(1)}, f32[136,128]{1,0:T(8,128)S(1)}, u32[]{:S(2)}, u32[]{:S(2)}) collective-permute-start(f32[136,128]{1,0:T(8,128)S(1)} %add_add_fusion.2), channel_id=1, source_target_pairs={{0,3},{1,0},{2,1},{3,2},{4,7},{5,4},{6,5},{7,6},{8,11},{9,8},{10,9... | collective-permute-start | bytes 208904 | tf_op jit(solution)/shard_map/ppermute | solution.py:290
  22.5 5.1 %collective-permute-start.5 = (f32[136,128]{1,0:T(8,128)S(1)}, f32[136,128]{1,0:T(8,128)S(1)}, u32[]{:S(2)}, u32[]{:S(2)}) collective-permute-start(f32[136,128]{1,0:T(8,128)S(1)} %add_add_fusion.2), channel_id=1, source_target_pairs={{0,1},{1,2},{2,3},{3,0},{4,5},{5,6},{6,7},{7,4},{8,9},{9,10},{10,1... | collective-permute-start | bytes 208904 | tf_op jit(solution)/shard_map/ppermute | solution.py:290
  22.5 5.1 %collective-permute-start.4 = (f32[136,128]{1,0:T(8,128)S(1)}, f32[136,128]{1,0:T(8,128)S(1)}, u32[]{:S(2)}, u32[]{:S(2)}) collective-permute-start(f32[136,128]{1,0:T(8,128)S(1)} %add_add_fusion.2), channel_id=1, source_target_pairs={{0,2},{1,3},{2,0},{3,1},{4,6},{5,7},{6,4},{7,5},{8,10},{9,11},{10,... | collective-permute-start | bytes 208904 | tf_op jit(solution)/shard_map/ppermute | solution.py:290
  27.7 5.2 %collective-permute-start.9 = (f32[136,128]{1,0:T(8,128)S(1)}, f32[136,128]{1,0:T(8,128)S(1)}, u32[]{:S(2)}, u32[]{:S(2)}) collective-permute-start(f32[136,128]{1,0:T(8,128)S(1)} %add_add_fusion.1), channel_id=1, source_target_pairs={{0,12},{1,13},{2,14},{3,15},{4,0},{5,1},{6,2},{7,3},{8,4},{9,5},{1... | collective-permute-start | bytes 208904 | tf_op jit(solution)/shard_map/ppermute | solution.py:290
  31.5 5.1 %collective-permute-start.8 = (f32[136,128]{1,0:T(8,128)S(1)}, f32[136,128]{1,0:T(8,128)S(1)}, u32[]{:S(2)}, u32[]{:S(2)}) collective-permute-start(f32[136,128]{1,0:T(8,128)S(1)} %add_add_fusion.1), channel_id=1, source_target_pairs={{0,4},{1,5},{2,6},{3,7},{4,8},{5,9},{6,10},{7,11},{8,12},{9,13},{1... | collective-permute-start | bytes 208904 | tf_op jit(solution)/shard_map/ppermute | solution.py:290
  31.5 5.1 %collective-permute-start.7 = (f32[136,128]{1,0:T(8,128)S(1)}, f32[136,128]{1,0:T(8,128)S(1)}, u32[]{:S(2)}, u32[]{:S(2)}) collective-permute-start(f32[136,128]{1,0:T(8,128)S(1)} %add_add_fusion.1), channel_id=1, source_target_pairs={{0,8},{1,9},{2,10},{3,11},{4,12},{5,13},{6,14},{7,15},{8,0},{9,1},... | collective-permute-start | bytes 208904 | tf_op jit(solution)/shard_map/ppermute | solution.py:290
  36.6 5.7 %collective-permute-start.10 = (f32[136,128]{1,0:T(8,128)S(1)}, f32[136,128]{1,0:T(8,128)S(1)}, u32[]{:S(2)}, u32[]{:S(2)}) collective-permute-start(f32[136,128]{1,0:T(8,128)S(1)} %add_add_fusion.mine_ref), channel_id=1, source_target_pairs={{0,16},{16,0},{32,48},{48,32},{64,80},{80,64},{96,112},{112,96},{1... | collective-permute-start | bytes 208904 | tf_op jit(solution)/shard_map/ppermute | solution.py:290

commit v5 on v4

--- a/solution.py
+++ b/solution.py
@@ -11,7 +11,7 @@
 SWEEPS = 3
 EARLY_TILES = 3
 MODES = 128
-GRAM_PARTS = 8
+GRAM_PARTS = 4
 APPLY_PARTS = 16
 GRAM_VMEM = 8 << 20
 CORE_VMEM = 8 << 20
@@ -220,10 +220,12 @@
             project = jnp.where(chosen, dot_nn(coeff, gram_all[:, MODES:], HIGHEST), 0.0)
         project_t = project.T
         own = jnp.where(chosen, identity, 0.0)
-        remainder = (
-            jnp.concatenate([jnp.zeros((MODES, MODES), F32), own], 1)
-            - dot_nn(project_t, coeff, HIGHEST)
-        )
+        if batch == 0:
+            remainder = jnp.concatenate([-project_t, own], 1)
+        else:
+            remainder = jnp.concatenate(
+                [jnp.zeros((MODES, MODES), F32), own], 1
+            ) - dot_nn(project_t, coeff, HIGHEST)
         gram = dot_nt(dot_nn(remainder, gram_all, HIGHEST), remainder, HIGHEST)
         low = batch * width
         head = jnp.where(row == lane, squares, 0.0) + dot_nn(project, project_t, HIGHEST)

time: 78.5 us -> 78.2 us (level)
  no operation moved by 1% of the time
where the time goes in v5:
time: 78.2 us; the launch traced here: 78.1 us
  Pallas kernels  43.3 us (55%)
  starting transfers between devices  20.2 us (26%)
  waiting for transfers between devices  13 us (17%)
  between operations  1.5 us (2%)
    pallas_call x1, Pallas kernels, core_call(): pl.pallas_call(functools.partial(core_kernel, batches), in_specs=[VMEM, V...  31.2 us
    ppermute x11, starting transfers between devices, exchange(): return lax.ppermute(array, axis, [(i, move(i)) for i in range(size)])  20.2 us
    ppermute x11, waiting for transfers between devices, exchange(): return lax.ppermute(array, axis, [(i, move(i)) for i in range(size)])  13 us
    pallas_call x1, Pallas kernels, gram_call(): pl.pallas_call(gram_kernel, in_specs=[SMEM, ANYWHERE, ANYWHERE], out_spec...  7.59 us
    pallas_call x1, Pallas kernels, apply_call(): pl.pallas_call(apply_kernel, in_specs=[SMEM, VMEM, VMEM, VMEM], out_specs...  4.57 us
  transfers between devices with their start and end apart: 11, of which 7 were waited for; matrix products, arithmetic and copies ran while one was open for 0% of the time, Pallas kernels for 0%

profile of v5, /device:TPU:1, one launch (start us, length us, event | category | flops | bytes accessed | tf_op | source)
XLA Modules:
  0.0 78.1 jit_solution(16062455653717558288)
XLA Ops:
  1.3 0.0 copy-start
  1.3 7.6 %gram.1 = (f32[136,128]{1,0:T(8,128)S(1)}, f32[136,128]{1,0:T(8,128)S(1)}, f32[128,16384]{1,0:T(8,128)S(1)}, f32[128,16384]{1,0:T(8,128)S(1)}) custom-call(s32[1]{0:T(128)S(6)} %copy.6.wet_ref, f32[128,16384]{1,0:T(8,128)} %basis_hbm.1, f32[128,16384]{1,0:T(8,128)} %bitcast.4), custom_call_target="tpu_custom_call" | custom-call | tf_op jit(solution)/shard_map/gram/pallas_call | solution.py:321
  8.9 1.5 %collective-permute-start = (f32[136,128]{1,0:T(8,128)S(1)}, f32[136,128]{1,0:T(8,128)S(1)}, u32[]{:S(2)}, u32[]{:S(2)}) collective-permute-start(f32[136,128]{1,0:T(8,128)S(1)} %get-tuple-element.9), channel_id=1, source_target_pairs={{0,16},{16,0},{32,48},{48,32},{64,80},{80,64},{96,112},{112,96},{1... | collective-permute-start | bytes 208904 | tf_op jit(solution)/shard_map/ppermute | solution.py:292
  10.3 0.9 %collective-permute-done = f32[136,128]{1,0:T(8,128)S(1)} collective-permute-done((f32[136,128]{1,0:T(8,128)S(1)}, f32[136,128]{1,0:T(8,128)S(1)}, u32[]{:S(2)}, u32[]{:S(2)}) %collective-permute-start) | collective-permute-done | bytes 69664 | tf_op jit(solution)/shard_map/ppermute | solution.py:292
  11.3 2.9 %collective-permute-start.3 = (f32[136,128]{1,0:T(8,128)S(1)}, f32[136,128]{1,0:T(8,128)S(1)}, u32[]{:S(2)}, u32[]{:S(2)}) collective-permute-start(f32[136,128]{1,0:T(8,128)S(1)} %add.30), channel_id=1, source_target_pairs={{0,96},{16,112},{32,0},{48,16},{64,32},{80,48},{96,64},{112,80},{1... | collective-permute-start | bytes 208904 | tf_op jit(solution)/shard_map/ppermute | solution.py:292
  14.2 0.0 collective-permute-start.2
  14.2 1.6 %collective-permute-start.1 = (f32[136,128]{1,0:T(8,128)S(1)}, f32[136,128]{1,0:T(8,128)S(1)}, u32[]{:S(2)}, u32[]{:S(2)}) collective-permute-start(f32[136,128]{1,0:T(8,128)S(1)} %add.30), channel_id=1, source_target_pairs={{0,64},{16,80},{32,96},{48,112},{64,0},{80,16},{96,32},{112,48},{1... | collective-permute-start | bytes 208904 | tf_op jit(solution)/shard_map/ppermute | solution.py:292
  15.8 0.0 collective-permute-done.3
  15.8 3.6 %collective-permute-done.2 = f32[136,128]{1,0:T(8,128)S(1)} collective-permute-done((f32[136,128]{1,0:T(8,128)S(1)}, f32[136,128]{1,0:T(8,128)S(1)}, u32[]{:S(2)}, u32[]{:S(2)}) %collective-permute-start.2) | collective-permute-done | bytes 69664 | tf_op jit(solution)/shard_map/ppermute | solution.py:292
  19.4 0.4 collective-permute-done.1
  19.8 2.5 %collective-permute-start.6 = (f32[136,128]{1,0:T(8,128)S(1)}, f32[136,128]{1,0:T(8,128)S(1)}, u32[]{:S(2)}, u32[]{:S(2)}) collective-permute-start(f32[136,128]{1,0:T(8,128)S(1)} %add_add_fusion.2), channel_id=1, source_target_pairs={{0,3},{1,0},{2,1},{3,2},{4,7},{5,4},{6,5},{7,6},{8,11},{9,8},{10,9... | collective-permute-start | bytes 208904 | tf_op jit(solution)/shard_map/ppermute | solution.py:292
  22.4 0.0 collective-permute-start.5
  22.4 1.7 %collective-permute-start.4 = (f32[136,128]{1,0:T(8,128)S(1)}, f32[136,128]{1,0:T(8,128)S(1)}, u32[]{:S(2)}, u32[]{:S(2)}) collective-permute-start(f32[136,128]{1,0:T(8,128)S(1)} %add_add_fusion.2), channel_id=1, source_target_pairs={{0,2},{1,3},{2,0},{3,1},{4,6},{5,7},{6,4},{7,5},{8,10},{9,11},{10,... | collective-permute-start | bytes 208904 | tf_op jit(solution)/shard_map/ppermute | solution.py:292
  24.1 0.0 collective-permute-done.6
  24.1 3.4 %collective-permute-done.5 = f32[136,128]{1,0:T(8,128)S(1)} collective-permute-done((f32[136,128]{1,0:T(8,128)S(1)}, f32[136,128]{1,0:T(8,128)S(1)}, u32[]{:S(2)}, u32[]{:S(2)}) %collective-permute-start.5) | collective-permute-done | bytes 69664 | tf_op jit(solution)/shard_map/ppermute | solution.py:292
  27.5 0.0 collective-permute-done.4
  27.5 3.8 %collective-permute-start.9 = (f32[136,128]{1,0:T(8,128)S(1)}, f32[136,128]{1,0:T(8,128)S(1)}, u32[]{:S(2)}, u32[]{:S(2)}) collective-permute-start(f32[136,128]{1,0:T(8,128)S(1)} %add_add_fusion.1), channel_id=1, source_target_pairs={{0,12},{1,13},{2,14},{3,15},{4,0},{5,1},{6,2},{7,3},{8,4},{9,5},{1... | collective-permute-start | bytes 208904 | tf_op jit(solution)/shard_map/ppermute | solution.py:292
  31.3 0.0 collective-permute-start.8
  31.4 1.3 %collective-permute-start.7 = (f32[136,128]{1,0:T(8,128)S(1)}, f32[136,128]{1,0:T(8,128)S(1)}, u32[]{:S(2)}, u32[]{:S(2)}) collective-permute-start(f32[136,128]{1,0:T(8,128)S(1)} %add_add_fusion.1), channel_id=1, source_target_pairs={{0,8},{1,9},{2,10},{3,11},{4,12},{5,13},{6,14},{7,15},{8,0},{9,1},... | collective-permute-start | bytes 208904 | tf_op jit(solution)/shard_map/ppermute | solution.py:292
  32.7 0.1 collective-permute-done.9
  32.7 3.7 %collective-permute-done.8 = f32[136,128]{1,0:T(8,128)S(1)} collective-permute-done((f32[136,128]{1,0:T(8,128)S(1)}, f32[136,128]{1,0:T(8,128)S(1)}, u32[]{:S(2)}, u32[]{:S(2)}) %collective-permute-start.8) | collective-permute-done | bytes 69664 | tf_op jit(solution)/shard_map/ppermute | solution.py:292
  36.5 0.0 collective-permute-done.7
  36.5 4.8 %collective-permute-start.10 = (f32[136,128]{1,0:T(8,128)S(1)}, f32[136,128]{1,0:T(8,128)S(1)}, u32[]{:S(2)}, u32[]{:S(2)}) collective-permute-start(f32[136,128]{1,0:T(8,128)S(1)} %add_add_fusion.mine_ref), channel_id=1, source_target_pairs={{0,16},{16,0},{32,48},{48,32},{64,80},{80,64},{96,112},{112,96},{1... | collective-permute-start | bytes 208904 | tf_op jit(solution)/shard_map/ppermute | solution.py:292
  41.3 0.9 %collective-permute-done.10.other_ref = f32[136,128]{1,0:T(8,128)S(1)} collective-permute-done((f32[136,128]{1,0:T(8,128)S(1)}, f32[136,128]{1,0:T(8,128)S(1)}, u32[]{:S(2)}, u32[]{:S(2)}) %collective-permute-start.10) | collective-permute-done | bytes 69664 | tf_op jit(solution)/shard_map/ppermute | solution.py:292
  42.2 0.0 copy-done
  42.2 31.2 %core.1 = (bf16[256,256]{1,0:T(8,128)(2,1)S(1)}, f32[1,128]{1,0:T(1,128)}) custom-call(f32[136,128]{1,0:T(8,128)S(1)} %add_add_fusion.mine_ref, f32[136,128]{1,0:T(8,128)S(1)} %collective-permute-done.10.other_ref, f32[1,128]{1,0:T(1,128)S(1)} %bitcast.3), custom_call_target="tpu_custom_call" | custom-call | tf_op jit(solution)/shard_map/core/pallas_call | solution.py:338
  73.3 4.6 %apply.1 = f32[128,16384]{1,0:T(8,128)} custom-call(s32[1]{0:T(128)S(6)} %copy.6.wet_ref, bf16[256,256]{1,0:T(8,128)(2,1)S(1)} %get-tuple-element.10.coeff_ref, f32[128,16384]{1,0:T(8,128)S(1)} %get-tuple-element.11.basis_ref, f32[128,16384]{1,0:T(8,128)S(1)} %get-tuple-element.12.snap_ref), custom_call_target="tpu_custom_call" | custom-call | tf_op jit(solution)/shard_map/apply/pallas_call | solution.py:354
  (4 shorter events, 0.1 us)
Async XLA Ops:
  1.3 40.9 %copy-start = (f32[128]{0:T(128)S(1)}, f32[128]{0:T(128)}, u32[]{:S(2)}) copy-start(f32[128]{0:T(128)} %param.5) | copy-start | bytes 1540
  8.9 2.4 %collective-permute-start = (f32[136,128]{1,0:T(8,128)S(1)}, f32[136,128]{1,0:T(8,128)S(1)}, u32[]{:S(2)}, u32[]{:S(2)}) collective-permute-start(f32[136,128]{1,0:T(8,128)S(1)} %get-tuple-element.9), channel_id=1, source_target_pairs={{0,16},{16,0},{32,48},{48,32},{64,80},{80,64},{96,112},{112,96},{1... | collective-permute-start | bytes 208904 | tf_op jit(solution)/shard_map/ppermute | solution.py:292
  11.3 4.6 %collective-permute-start.3 = (f32[136,128]{1,0:T(8,128)S(1)}, f32[136,128]{1,0:T(8,128)S(1)}, u32[]{:S(2)}, u32[]{:S(2)}) collective-permute-start(f32[136,128]{1,0:T(8,128)S(1)} %add.30), channel_id=1, source_target_pairs={{0,96},{16,112},{32,0},{48,16},{64,32},{80,48},{96,64},{112,80},{1... | collective-permute-start | bytes 208904 | tf_op jit(solution)/shard_map/ppermute | solution.py:292
  14.2 5.2 %collective-permute-start.2 = (f32[136,128]{1,0:T(8,128)S(1)}, f32[136,128]{1,0:T(8,128)S(1)}, u32[]{:S(2)}, u32[]{:S(2)}) collective-permute-start(f32[136,128]{1,0:T(8,128)S(1)} %add.30), channel_id=1, source_target_pairs={{0,32},{16,48},{32,64},{48,80},{64,96},{80,112},{96,0},{112,16},{1... | collective-permute-start | bytes 208904 | tf_op jit(solution)/shard_map/ppermute | solution.py:292
  14.2 5.6 %collective-permute-start.1 = (f32[136,128]{1,0:T(8,128)S(1)}, f32[136,128]{1,0:T(8,128)S(1)}, u32[]{:S(2)}, u32[]{:S(2)}) collective-permute-start(f32[136,128]{1,0:T(8,128)S(1)} %add.30), channel_id=1, source_target_pairs={{0,64},{16,80},{32,96},{48,112},{64,0},{80,16},{96,32},{112,48},{1... | collective-permute-start | bytes 208904 | tf_op jit(solution)/shard_map/ppermute | solution.py:292
  19.8 4.3 %collective-permute-start.6 = (f32[136,128]{1,0:T(8,128)S(1)}, f32[136,128]{1,0:T(8,128)S(1)}, u32[]{:S(2)}, u32[]{:S(2)}) collective-permute-start(f32[136,128]{1,0:T(8,128)S(1)} %add_add_fusion.2), channel_id=1, source_target_pairs={{0,3},{1,0},{2,1},{3,2},{4,7},{5,4},{6,5},{7,6},{8,11},{9,8},{10,9... | collective-permute-start | bytes 208904 | tf_op jit(solution)/shard_map/ppermute | solution.py:292
  22.4 5.1 %collective-permute-start.5 = (f32[136,128]{1,0:T(8,128)S(1)}, f32[136,128]{1,0:T(8,128)S(1)}, u32[]{:S(2)}, u32[]{:S(2)}) collective-permute-start(f32[136,128]{1,0:T(8,128)S(1)} %add_add_fusion.2), channel_id=1, source_target_pairs={{0,1},{1,2},{2,3},{3,0},{4,5},{5,6},{6,7},{7,4},{8,9},{9,10},{10,1... | collective-permute-start | bytes 208904 | tf_op jit(solution)/shard_map/ppermute | solution.py:292
  22.4 5.1 %collective-permute-start.4 = (f32[136,128]{1,0:T(8,128)S(1)}, f32[136,128]{1,0:T(8,128)S(1)}, u32[]{:S(2)}, u32[]{:S(2)}) collective-permute-start(f32[136,128]{1,0:T(8,128)S(1)} %add_add_fusion.2), channel_id=1, source_target_pairs={{0,2},{1,3},{2,0},{3,1},{4,6},{5,7},{6,4},{7,5},{8,10},{9,11},{10,... | collective-permute-start | bytes 208904 | tf_op jit(solution)/shard_map/ppermute | solution.py:292
  27.5 5.2 %collective-permute-start.9 = (f32[136,128]{1,0:T(8,128)S(1)}, f32[136,128]{1,0:T(8,128)S(1)}, u32[]{:S(2)}, u32[]{:S(2)}) collective-permute-start(f32[136,128]{1,0:T(8,128)S(1)} %add_add_fusion.1), channel_id=1, source_target_pairs={{0,12},{1,13},{2,14},{3,15},{4,0},{5,1},{6,2},{7,3},{8,4},{9,5},{1... | collective-permute-start | bytes 208904 | tf_op jit(solution)/shard_map/ppermute | solution.py:292
  31.3 5.1 %collective-permute-start.8 = (f32[136,128]{1,0:T(8,128)S(1)}, f32[136,128]{1,0:T(8,128)S(1)}, u32[]{:S(2)}, u32[]{:S(2)}) collective-permute-start(f32[136,128]{1,0:T(8,128)S(1)} %add_add_fusion.1), channel_id=1, source_target_pairs={{0,4},{1,5},{2,6},{3,7},{4,8},{5,9},{6,10},{7,11},{8,12},{9,13},{1... | collective-permute-start | bytes 208904 | tf_op jit(solution)/shard_map/ppermute | solution.py:292
  31.4 5.1 %collective-permute-start.7 = (f32[136,128]{1,0:T(8,128)S(1)}, f32[136,128]{1,0:T(8,128)S(1)}, u32[]{:S(2)}, u32[]{:S(2)}) collective-permute-start(f32[136,128]{1,0:T(8,128)S(1)} %add_add_fusion.1), channel_id=1, source_target_pairs={{0,8},{1,9},{2,10},{3,11},{4,12},{5,13},{6,14},{7,15},{8,0},{9,1},... | collective-permute-start | bytes 208904 | tf_op jit(solution)/shard_map/ppermute | solution.py:292
  36.5 5.7 %collective-permute-start.10 = (f32[136,128]{1,0:T(8,128)S(1)}, f32[136,128]{1,0:T(8,128)S(1)}, u32[]{:S(2)}, u32[]{:S(2)}) collective-permute-start(f32[136,128]{1,0:T(8,128)S(1)} %add_add_fusion.mine_ref), channel_id=1, source_target_pairs={{0,16},{16,0},{32,48},{48,32},{64,80},{80,64},{96,112},{112,96},{1... | collective-permute-start | bytes 208904 | tf_op jit(solution)/shard_map/ppermute | solution.py:292
